TPU v7x, 256 devices: a whole 4x4x8 slice. The times are simulated.
256 devices in a mesh: col: 8 (over z), bulk: 32 (over y, x, core).
Axes of the slice: x: 4, y: 4, z: 8, core: 2. Of those that a mesh axis runs over, the one named last changes fastest.
Arguments:
- block_input_field: bfloat16 [96, 4, 64, 1024], P(None, None, 'bulk', 'col'), may hold values from -128 to 128
- upstream_derivative: bfloat16 [96, 4, 64, 1024], P(None, None, 'bulk', 'col'), may hold values from -8 to 8
- pointwise_mixing_matrix: bfloat16 [288, 96], replicated, may hold values from -0.625 to 0.625
- per_channel_kernel: float32 [288, 27], replicated, may hold values from -1.25 to 1.25
- sharpness_per_group: float32 [2], replicated, may hold values from 0.5 to 4
Outputs:
- block_input_derivative: bfloat16 [96, 4, 64, 1024], P(None, None, 'bulk', 'col')
- pointwise_mixing_derivative: float32 [288, 96], replicated
- per_channel_kernel_derivative: float32 [288, 27], replicated
- sharpness_derivative: float32 [2], replicated
All inputs are finite; a program needn't handle non-finite values.
Results may differ from a plain program's by a relative error of at most 0.00165.
The roundings to bfloat16 on the way count: a program that leaves them out, or rounds other values in their place, can miss the bound.
Values may be sent and summed in bfloat16 or wider, within the bound.
A program may use at most 64 MiB of HBM per device.

v0:
```python
import math

import jax
import jax.numpy as jnp
from jax import lax
from jax.sharding import PartitionSpec as P


def extended(cells, sides, width):
    for axis, dim in sides:
        count = lax.axis_size(axis)
        ends = count - 1
        head = lax.slice_in_dim(cells, 0, width, axis=dim)
        tail = lax.slice_in_dim(cells, cells.shape[dim] - width, cells.shape[dim], axis=dim)
        cells = jnp.concatenate(
            [
                lax.ppermute(tail, axis, [(i, (i + 1) % count) for i in range(ends)]),
                cells,
                lax.ppermute(head, axis, [((i + 1) % count, i) for i in range(ends)]),
            ],
            axis=dim,
        )
    return cells


def depth_apply(padded, weights, array_shape, flip):
    depth_z, rows_y, cols_x = array_shape
    total = jnp.zeros((padded.shape[0], depth_z, rows_y, cols_x), jnp.float32)
    for shift_z in range(3):
        for shift_y in range(3):
            for shift_x in range(3):
                tap = 9 * shift_z + 3 * shift_y + shift_x
                if flip:
                    start_z, start_y, start_x = (2 - shift_z, 2 - shift_y, 2 - shift_x)
                else:
                    start_z, start_y, start_x = (shift_z, shift_y, shift_x)
                window = padded[
                    :,
                    start_z : start_z + depth_z,
                    start_y : start_y + rows_y,
                    start_x : start_x + cols_x,
                ]
                total = total + weights[:, tap][:, None, None, None] * window.astype(jnp.float32)
    return total


def depth_grad(padded, grads, array_shape):
    depth_z, rows_y, cols_x = array_shape
    grads_f = grads.astype(jnp.float32)
    columns = []
    for shift_z in range(3):
        for shift_y in range(3):
            for shift_x in range(3):
                window = padded[
                    :,
                    shift_z : shift_z + depth_z,
                    shift_y : shift_y + rows_y,
                    shift_x : shift_x + cols_x,
                ]
                columns.append(jnp.sum(grads_f * window.astype(jnp.float32), axis=(1, 2, 3)))
    return jnp.stack(columns, axis=1)


def pad_planes(field):
    return jnp.pad(field, ((0, 0), (1, 1), (0, 0), (0, 0)))


def head_grads(
    mixed_flat,
    cot_flat,
    coupling,
    attention,
    inv_query,
    inv_keys,
    diag_query,
    diag_keys,
    group_sequence,
    head_dim,
):
    channels = group_sequence * head_dim
    width = mixed_flat.shape[1]
    q_heads = mixed_flat[:channels].reshape(group_sequence, head_dim, width)
    k_heads = mixed_flat[channels : 2 * channels].reshape(group_sequence, head_dim, width)
    g_heads = cot_flat.reshape(group_sequence, head_dim, width)
    query_term = jnp.einsum("hij,hjv->hiv", coupling, k_heads, preferred_element_type=jnp.float32)
    keys_term = jnp.einsum("hij,hiv->hjv", coupling, q_heads, preferred_element_type=jnp.float32)
    grad_query = query_term - (inv_query * inv_query * diag_query)[:, :, None] * q_heads.astype(
        jnp.float32
    )
    grad_keys = keys_term - (inv_keys * inv_keys * diag_keys)[:, :, None] * k_heads.astype(
        jnp.float32
    )
    grad_values = jnp.einsum(
        "hij,hiv->hjv", attention.astype(jnp.bfloat16), g_heads, preferred_element_type=jnp.float32
    )
    return jnp.concatenate(
        [
            grad_query.reshape(channels, width),
            grad_keys.reshape(channels, width),
            grad_values.reshape(channels, width),
        ],
        axis=0,
    )


def local(
    block_input_field,
    upstream_derivative,
    pointwise_mixing_matrix,
    per_channel_kernel,
    sharpness_per_group,
):
    channels = block_input_field.shape[0]
    group_sequence = sharpness_per_group.shape[0]
    head_dim = channels // group_sequence
    array_shape = block_input_field.shape[1:]
    depth_z, rows_y, cols_x = array_shape
    count = depth_z * rows_y * cols_x
    voxels = count * lax.axis_size("col") * lax.axis_size("bulk")
    multiplier_value = 1.0 / math.sqrt(voxels)
    flat_source = block_input_field.reshape(channels, count)
    extra = 1
    fields = jnp.dot(pointwise_mixing_matrix, flat_source, preferred_element_type=jnp.float32)
    fields = fields.astype(jnp.bfloat16).reshape((3 * channels,) + array_shape)
    border = extended(fields, (("col", 3), ("bulk", 2)), extra)
    ext_shape = (depth_z, rows_y + 2 * extra - 2, cols_x + 2 * extra - 2)
    mixed_ext = depth_apply(pad_planes(border), per_channel_kernel, ext_shape, False).astype(
        jnp.bfloat16
    )
    padded_field = pad_planes(border)
    flat_mixed = mixed_ext.reshape(3 * channels, count)
    query = flat_mixed[:channels]
    keys_block = flat_mixed[channels : 2 * channels]
    values = flat_mixed[2 * channels :]
    q_heads = query.reshape(group_sequence, head_dim, count)
    k_heads = keys_block.reshape(group_sequence, head_dim, count)
    v_heads = values.reshape(group_sequence, head_dim, count)
    g_heads = upstream_derivative.reshape(group_sequence, head_dim, count)
    sq_query = jnp.sum(jnp.square(query.astype(jnp.float32)), axis=1)
    sq_keys = jnp.sum(jnp.square(keys_block.astype(jnp.float32)), axis=1)
    gram_local = jnp.einsum("hiv,hjv->hij", q_heads, k_heads, preferred_element_type=jnp.float32)
    value_local = jnp.einsum("hiv,hjv->hij", g_heads, v_heads, preferred_element_type=jnp.float32)
    sq_query, sq_keys, gram, value_grad = lax.psum(
        (sq_query, sq_keys, gram_local, value_local), ("col", "bulk")
    )
    inv_query = (1.0 / jnp.sqrt(sq_query + 1e-06)).reshape(group_sequence, head_dim)
    inv_keys = (1.0 / jnp.sqrt(sq_keys + 1e-06)).reshape(group_sequence, head_dim)
    normalized_similarities = gram * inv_query[:, :, None] * inv_keys[:, None, :]
    softmax_numerators = jnp.exp(sharpness_per_group[:, None, None] * normalized_similarities)
    attention = softmax_numerators / jnp.sum(softmax_numerators, axis=2, keepdims=True)
    logit_derivative = attention * (
        value_grad - jnp.sum(attention * value_grad, axis=2, keepdims=True)
    )
    sharpness_derivative = (
        jnp.sum(logit_derivative * normalized_similarities, axis=(1, 2)) * multiplier_value
    )
    similarity_derivative = sharpness_per_group[:, None, None] * logit_derivative
    diag_query = jnp.sum(similarity_derivative * normalized_similarities, axis=2)
    diag_keys = jnp.sum(similarity_derivative * normalized_similarities, axis=1)
    coupling = (inv_query[:, :, None] * similarity_derivative * inv_keys[:, None, :]).astype(
        jnp.bfloat16
    )
    grads_flat = head_grads(
        flat_mixed,
        upstream_derivative.reshape(channels, count),
        coupling,
        attention,
        inv_query,
        inv_keys,
        diag_query,
        diag_keys,
        group_sequence,
        head_dim,
    )
    mixed_grad = grads_flat.astype(jnp.bfloat16).reshape((3 * channels,) + array_shape)
    grad_border = extended(mixed_grad, (("col", 3), ("bulk", 2)), 1)
    field_grad = depth_apply(pad_planes(grad_border), per_channel_kernel, array_shape, True).astype(
        jnp.bfloat16
    )
    depth_local = depth_grad(padded_field, mixed_grad, array_shape)
    flat_grad = field_grad.reshape(3 * channels, count)
    weight_local = lax.dot_general(
        flat_grad, flat_source, (((1,), (1,)), ((), ())), preferred_element_type=jnp.float32
    )
    source_gradient_part = lax.dot_general(
        pointwise_mixing_matrix,
        flat_grad,
        (((0,), (0,)), ((), ())),
        preferred_element_type=jnp.float32,
    )
    source_gradient_part = source_gradient_part.astype(jnp.bfloat16).reshape(
        block_input_field.shape
    )
    weight_grand_total, depthwise_total = lax.psum((weight_local, depth_local), ("col", "bulk"))
    return (
        source_gradient_part,
        weight_grand_total * multiplier_value,
        depthwise_total * multiplier_value,
        sharpness_derivative,
    )


def solution(mesh):
    return jax.shard_map(
        local,
        mesh=mesh,
        in_specs=(P(None, None, "bulk", "col"), P(None, None, "bulk", "col"), P(), P(), P()),
        out_specs=(P(None, None, "bulk", "col"), P(), P(), P()),
        check_vma=False,
    )
```

profile of v0, /device:TPU:1, one launch (start us, length us, event | category | flops | bytes accessed | tf_op | source)
XLA Modules:
  0.0 516.0 jit_solution(14994292413712869115)
XLA Ops:
  7.2 1.0 reshape.113
  9.0 1.1 fusion.114
  10.1 0.7 copy.77
  10.8 4.4 collective-permute-start
  15.2 0.7 copy.78
  15.9 1.3 collective-permute-start.1
  17.6 2.8 collective-permute-done.1
  20.8 0.7 pad_maximum_fusion.2
  21.6 1.1 copy.83
  22.7 3.8 collective-permute-start.3
  26.5 1.1 copy.82
  27.6 3.0 collective-permute-start.2
  30.9 2.4 collective-permute-done.3
  33.7 2.0 collective-permute-done.2
  35.7 1.3 copy.84
  37.0 1.3 fusion.11
  38.3 2.1 maximum_maximum_fusion
  40.5 5.8 %fusion.42 = bf16[288,4,2,128]{3,0,2,1:T(8,128)(2,1)S(1)} fusion(bf16[288,4,2,128]{3,0,2,1:T(8,128)(2,1)S(1)} %copy.80, f32[288]{0:T(512)S(1)} %get-tuple-element.65, f32[288]{0:T(512)S(1)} %get-tuple-element.66, f32[288]{0:T(512)S(1)} %get-tuple-element.41, f32[288]{0:T(512)S(1)} %get-tuple-element.42, f32[288]{0:T(512)S(1)} %get-tuple-element.43, ...), kind=kLoop, calls=%fused_computation.106 | loop fusion | flops 25657344 | bytes 15375744 | tf_op jit(solution)/shard_map/convert_element_type | solution.py:127
  47.9 83.4 %all-reduce.2 = (f32[96]{0:T(128)S(1)}, f32[2,48,48]{2,1,0:T(8,128)S(1)}, f32[96]{0:T(128)S(1)}, f32[2,48,48]{2,1,0:T(8,128)S(1)}) all-reduce(f32[96]{0:T(128)S(1)} %get-tuple-element.36, f32[2,48,48]{2,1,0:T(8,128)S(1)} %fusion.115, f32[96]{0:T(128)S(1)} %get-tuple-element.35, ...), channel_id=1, replica_groups=mesh['col'=8,'bulk'=32] {'col','bulk'}, use_global_device_ids=true, to_apply=%region_4.5 | all-reduce | flops 9408 | bytes 75264 | tf_op jit(solution)/shard_map/psum | solution.py:143
  132.0 0.9 fusion.94
  134.8 5.8 %fusion.73 = (f32[288]{0:T(512)}, f32[288]{0:T(512)}, f32[288]{0:T(512)}, f32[288]{0:T(512)}, f32[288]{0:T(512)}, /*index=5*/f32[288]{0:T(512)}, f32[288]{0:T(512)}, f32[288]{0:T(512)S(1)}) fusion(bf16[288,4,2,128]{3,0,2,1:T(8,128)(2,1)S(1)} %copy_dynamic-update-slice_fusion, bf16[288,4,3,130]{3,0,2,1:T(8,128)(2,1)} %copy-done.4, ...), kind=kLoop, calls=%fused_computation.137 | loop fusion | flops 9139968 | bytes 4737024 | tf_op jit(solution)/shard_map/reduce_sum | solution.py:60
  140.5 5.2 %fusion.82 = (f32[288]{0:T(512)}, f32[288]{0:T(512)}, f32[288]{0:T(512)}, f32[288]{0:T(512)}, f32[288]{0:T(512)}, /*index=5*/f32[288]{0:T(512)}, f32[288]{0:T(51...) fusion(bf16[288,4,2,128]{3,0,2,1:T(8,128)(2,1)S(1)} %copy_dynam, ...), kind=kLoop, calls=%fused_computation.146 | loop fusion | flops 16214976 | bytes 11227392 | tf_op jit(solution)/shard_map/reduce_sum | solution.py:60
  146.6 1.3 collective-permute-start.5
  147.9 4.0 collective-permute-start.4
  153.4 0.7 pad_maximum_fusion.3
  154.1 0.9 fusion.110
  155.0 2.2 copy.106
  157.2 1.1 copy.107
  158.2 4.2 collective-permute-start.7
  162.5 1.9 collective-permute-start.6
  164.4 1.2 multiply_reduce_fusion
  165.6 0.7 stack.110
  166.3 0.7 stack.101
  169.0 0.7 stack.93
  169.6 0.7 stack.95
  171.0 0.7 stack.86
  171.7 0.7 stack.87
  173.0 0.7 stack.89
  173.7 0.7 stack.90
  175.2 75.4 %psum.47 = f32[288,27]{0,1:T(8,128)S(1)} all-reduce(f32[288,27]{0,1:T(8,128)S(1)} %stack.111), channel_id=1, replica_groups=mesh['col'=8,'bulk'=32] {'col','bulk'}, use_global_device_ids=true, to_apply=%region_38.39 | all-reduce | flops 7776 | bytes 62208 | tf_op jit(solution)/shard_map/psum | solution.py:194
  251.6 1.3 copy.108
  252.9 1.3 select_maximum_fusion
  254.3 2.1 pad_maximum_fusion.1
  256.5 5.9 %fusion.83 = bf16[288,4,2,128]{3,0,2,1:T(8,128)(2,1)S(1)} fusion(bf16[288,4,2,128]{3,0,2,1:T(8,128)(2,1)S(1)} %copy_dynamic-update-slice_fusion, bf16[288,6,4,130]{3,0,2,1:T(8,128)(2,1)S(1)} %select_maximum_fusion, bf16[288,4,3,130]{3,0,2,1:T(8,128)(2,1)S(1)} %get-tuple-element.72, bf16[288,4,2,1]{3,0,2,1:T(8,128)(2,1)S(1)} %copy.104, ...), kind=kLoop, calls=%fused_computation.150 | loop fusion | flops 25657344 | bytes 15375744 | tf_op jit(solution)/shard_map/convert_element_type | solution.py:177
  262.4 1.0 convolution_bitcast_fusion
  264.6 0.8 reshape.120
  265.4 242.2 %all-reduce.5.cloned.1.call-done = f32[288,96]{1,0:T(8,128)} async-done(((f32[288,96]{1,0:T(8,128)}), f32[288,96]{1,0:T(8,128)}) %all-reduce.5.cloned.1.call-update) | async-done | bytes 110608 | tf_op jit(solution)/shard_map/psum | solution.py:194
  507.6 1.6 broadcast_multiply_fusion
  (119 shorter events, 14.9 us)
Async XLA Ops:
  7.2 1.1 copy-start
  7.2 500.4 %all-reduce.5.cloned.1.call-start = ((), (), s32[]{:S(2)}) async-start(), calls=%async_computation | async-start | bytes 294912 | tf_op jit(solution)/shard_map/psum | solution.py:194
  8.6 1.5 copy-start.5
  10.8 6.5 %collective-permute-start = (bf16[288,4,2,1]{0,1,3,2:T(4,128)(2,1)S(1)}, bf16[288,4,2,1]{0,1,3,2:T(4,128)(2,1)S(1)}, u32[]{:S(2)}, u32[]{:S(2)}) collective-permute-start(bf16[288,4,2,1]{0,1,3,2:T(4,128)(2,1)S(1)} %copy.77), channel_id=1, source_target_pairs={{0,32},{32,64},{64,96},{96,128},{128,160},{160,192},{192,224},{1,3... | collective-permute-start | bytes 13832 | tf_op jit(solution)/shard_map/ppermute | solution.py:17
  15.9 4.5 collective-permute-start.1
  21.6 9.0 %copy-start.9 = (bf16[96,4,2,128]{3,2,1,0:T(2,128)(2,1)S(1)}, bf16[96,4,2,128]{3,2,1,0:T(2,128)(2,1)}, u32[]{:S(2)}) copy-start(bf16[96,4,2,128]{3,2,1,0:T(2,128)(2,1)} %param.6) | copy-start | bytes 589828
  21.6 9.1 %copy-start.10 = (f32[288,27]{0,1:T(8,128)S(1)}, f32[288,27]{0,1:T(8,128)}, u32[]{:S(2)}) copy-start(f32[288,27]{0,1:T(8,128)} %param.8) | copy-start | bytes 93316
  22.7 10.6 %collective-permute-start.3 = (bf16[288,4,1,130]{0,1,3,2:T(4,128)(2,1)}, bf16[288,4,1,130]{0,1,3,2:T(4,128)(2,1)S(1)}, u32[]{:S(2)}, u32[]{:S(2)}) collective-permute-start(bf16[288,4,1,130]{0,1,3,2:T(4,128)(2,1)} %copy.83), channel_id=1, source_target_pairs={{1,0},{2,1},{3,2},{4,3},{5,4},{6,5},{7,6},{8,7},{9,8},{10,9},{11,1... | collective-permute-start | bytes 898568 | tf_op jit(solution)/shard_map/ppermute | solution.py:19
  27.6 8.1 %collective-permute-start.2 = (bf16[288,4,1,130]{0,1,3,2:T(4,128)(2,1)}, bf16[288,4,1,130]{0,1,3,2:T(4,128)(2,1)}, u32[]{:S(2)}, u32[]{:S(2)}) collective-permute-start(bf16[288,4,1,130]{0,1,3,2:T(4,128)(2,1)} %copy.82), channel_id=1, source_target_pairs={{0,1},{1,2},{2,3},{3,4},{4,5},{5,6},{6,7},{7,8},{8,9},{9,10},{10,1... | collective-permute-start | bytes 898568 | tf_op jit(solution)/shard_map/ppermute | solution.py:17
  30.9 9.6 %copy-start.11 = (f32[288]{0:T(512)}, f32[288]{0:T(512)S(1)}, u32[]{:S(2)}) copy-start(f32[288]{0:T(512)S(1)} %get-tuple-element.54) | copy-start | bytes 3460
  30.9 9.6 %copy-start.13 = (f32[288]{0:T(512)}, f32[288]{0:T(512)S(1)}, u32[]{:S(2)}) copy-start(f32[288]{0:T(512)S(1)} %get-tuple-element.55) | copy-start | bytes 3460
  30.9 9.6 %copy-start.15 = (f32[288]{0:T(512)}, f32[288]{0:T(512)S(1)}, u32[]{:S(2)}) copy-start(f32[288]{0:T(512)S(1)} %get-tuple-element.56) | copy-start | bytes 3460
  30.9 9.6 %copy-start.17 = (f32[288]{0:T(512)}, f32[288]{0:T(512)S(1)}, u32[]{:S(2)}) copy-start(f32[288]{0:T(512)S(1)} %get-tuple-element.57) | copy-start | bytes 3460
  30.9 9.6 %copy-start.19 = (f32[288]{0:T(512)}, f32[288]{0:T(512)S(1)}, u32[]{:S(2)}) copy-start(f32[288]{0:T(512)S(1)} %get-tuple-element.58) | copy-start | bytes 3460
  38.3 2.2 copy-start.1
  40.5 5.9 %copy-start.3 = (bf16[288,4,3,130]{3,0,2,1:T(8,128)(2,1)}, bf16[288,4,3,130]{3,0,2,1:T(8,128)(2,1)S(1)}, u32[]{:S(2)}) copy-start(bf16[288,4,3,130]{3,0,2,1:T(8,128)(2,1)S(1)} %get-tuple-element.73) | copy-start | bytes 2695684
  40.5 5.9 %copy-start.4 = (bf16[288,4,3,130]{3,0,2,1:T(8,128)(2,1)}, bf16[288,4,3,130]{3,0,2,1:T(8,128)(2,1)S(1)}, u32[]{:S(2)}) copy-start(bf16[288,4,3,130]{3,0,2,1:T(8,128)(2,1)S(1)} %get-tuple-element.74) | copy-start | bytes 2695684
  47.1 84.4 %copy-start.21 = (f32[2]{0:T(128)S(1)}, f32[2]{0:T(128)}, u32[]{:S(2)}) copy-start(f32[2]{0:T(128)} %param.9) | copy-start | bytes 28
  133.8 0.7 copy-start.8
  134.7 5.8 %copy-start.2 = (bf16[288,6,4,130]{3,0,2,1:T(8,128)(2,1)S(1)}, bf16[288,6,4,130]{3,0,2,1:T(8,128)(2,1)}, u32[]{:S(2)}) copy-start(bf16[288,6,4,130]{3,0,2,1:T(8,128)(2,1)} %copy-done.1) | copy-start | bytes 5391364
  146.0 5.9 %copy-start.22 = (f32[2]{0:T(128)S(1)}, f32[2]{0:T(128)}, u32[]{:S(2)}) copy-start(f32[2]{0:T(128)} %get-tuple-element.39) | copy-start | bytes 28
  146.6 6.4 %collective-permute-start.5 = (bf16[288,4,2,1]{0,1,3,2:T(4,128)(2,1)S(1)}, bf16[288,4,2,1]{0,1,3,2:T(4,128)(2,1)S(1)}, u32[]{:S(2)}, u32[]{:S(2)}) collective-permute-start(bf16[288,4,2,1]{0,1,3,2:T(4,128)(2,1)S(1)} %copy.103), channel_id=1, source_target_pairs={{32,0},{64,32},{96,64},{128,96},{160,128},{192,160},{224,192},{33,... | collective-permute-start | bytes 13832 | tf_op jit(solution)/shard_map/ppermute | solution.py:19
  147.9 4.8 collective-permute-start.4
  155.0 9.4 %copy-start.6 = (bf16[288,1024]{1,0:T(8,128)(2,1)S(1)}, bf16[288,1024]{1,0:T(8,128)(2,1)}, u32[]{:S(2)}) copy-start(bf16[288,1024]{1,0:T(8,128)(2,1)} %copy-done.5) | copy-start | bytes 1769476
  158.2 93.0 %collective-permute-start.7 = (bf16[288,4,1,130]{0,1,3,2:T(4,128)(2,1)}, bf16[288,4,1,130]{0,1,3,2:T(4,128)(2,1)S(1)}, u32[]{:S(2)}, u32[]{:S(2)}) collective-permute-start(bf16[288,4,1,130]{0,1,3,2:T(4,128)(2,1)} %copy.107), channel_id=1, source_target_pairs={{1,0},{2,1},{3,2},{4,3},{5,4},{6,5},{7,6},{8,7},{9,8},{10,9},{11,1... | collective-permute-start | bytes 898568 | tf_op jit(solution)/shard_map/ppermute | solution.py:19
  162.5 89.1 %collective-permute-start.6 = (bf16[288,4,1,130]{0,1,3,2:T(4,128)(2,1)}, bf16[288,4,1,130]{0,1,3,2:T(4,128)(2,1)}, u32[]{:S(2)}, u32[]{:S(2)}) collective-permute-start(bf16[288,4,1,130]{0,1,3,2:T(4,128)(2,1)} %copy.106), channel_id=1, source_target_pairs={{0,1},{1,2},{2,3},{3,4},{4,5},{5,6},{6,7},{7,8},{8,9},{9,10},{10,1... | collective-permute-start | bytes 898568 | tf_op jit(solution)/shard_map/ppermute | solution.py:17
  254.2 2.2 copy-start.12
  254.3 2.2 copy-start.14
  254.3 2.2 copy-start.16
  254.3 2.2 copy-start.18
  254.3 2.2 copy-start.20
  256.5 5.9 %copy-start.7 = (bf16[96,4,2,128]{3,2,1,0:T(2,128)(2,1)S(1)}, bf16[96,4,2,128]{3,2,1,0:T(2,128)(2,1)}, u32[]{:S(2)}) copy-start(bf16[96,4,2,128]{3,2,1,0:T(2,128)(2,1)} %param.5) | copy-start | bytes 589828
Sparse Core Ops, SparseCore 0:
  264.4 243.1 all-reduce.4
where the time goes:
time: 517 us; the launch traced here: 516 us
  waiting for transfers between devices  250 us (48%)
  blocking collectives  159 us (31%)
  other arithmetic  36.2 us (7%)
  local copies, waits for them, and re-layouts  29.6 us (6%)
  starting transfers between devices  23.9 us (5%)
  between operations  14.8 us (3%)
    psum x1, waiting for transfers between devices, local(): lax.psum((weight_local, depth_local), ('col', 'bulk'))  242 us
    psum x1, blocking collectives, local(): lax.psum((sq_query, sq_keys, gram_local, value_local), ('col', 'bulk'))  83.4 us
    psum x1, blocking collectives, local(): lax.psum((weight_local, depth_local), ('col', 'bulk'))  75.4 us
    ppermute x4, starting transfers between devices, extended(): lax.ppermute(tail, axis, [(i, (i + 1) % count) for i in range(ends)])  13.3 us
    reduce_sum x3, other arithmetic, depth_grad(): jnp.sum(grads_f * window.astype(jnp.float32), axis=(1, 2, 3))  12.2 us
    ppermute x4, starting transfers between devices, extended(): lax.ppermute(head, axis, [((i + 1) % count, i) for i in range(ends)])  10.6 us
  transfers between devices with their start and end apart: 9, of which 5 were waited for; matrix products, arithmetic and copies ran while one was open for 3% of the time, Pallas kernels for 0%

commit v1 on v0

--- a/solution.py
+++ b/solution.py
@@ -1,9 +1,116 @@
+import functools
 import math
 
 import jax
 import jax.numpy as jnp
 from jax import lax
+from jax.experimental import pallas as pl
+from jax.experimental.pallas import tpu as pltpu
 from jax.sharding import PartitionSpec as P
+
+
+MESH = pl.DeviceIdType.MESH
+
+
+def ring_copy(src, dst, send, recv, target):
+    return pltpu.make_async_remote_copy(
+        src_ref=src, dst_ref=dst, send_sem=send, recv_sem=recv, device_id=target, device_id_type=MESH
+    )
+
+
+def reduce_kernel(
+    n_col, n_bulk, rows, x_ref, o_ref, pack, parts, planes, whole, s_send, s_recv, z_send, z_recv, g_send, g_recv
+):
+    col, bulk = lax.axis_index("col"), lax.axis_index("bulk")
+
+    def other_bulk(step):
+        return lax.rem(bulk + step, n_bulk)
+
+    def other_col(step):
+        return lax.rem(col + step, n_col)
+
+    barrier = pltpu.get_barrier_semaphore()
+
+    def greet_bulk(step, carry):
+        pl.semaphore_signal(barrier, inc=1, device_id=(col, other_bulk(step)), device_id_type=MESH)
+        return carry
+
+    def greet_col(step, carry):
+        pl.semaphore_signal(barrier, inc=1, device_id=(other_col(step), bulk), device_id_type=MESH)
+        return carry
+
+    lax.fori_loop(1, n_bulk, greet_bulk, 0)
+    lax.fori_loop(1, n_col, greet_col, 0)
+    for i in range(n_bulk):
+        pack[i] = x_ref[rows * i : rows * (i + 1), :]
+    pl.semaphore_wait(barrier, n_bulk + n_col - 2)
+
+    def scatter(step):
+        peer = other_bulk(step)
+        return ring_copy(pack.at[peer], parts.at[bulk], s_send.at[peer], s_recv.at[bulk], (col, peer))
+
+    def gathered(step):
+        peer = other_bulk(step)
+        return ring_copy(pack.at[peer], parts.at[peer], s_send.at[peer], s_recv.at[peer], (col, peer))
+
+    def across(step):
+        peer = other_col(step)
+        return ring_copy(planes.at[col], planes.at[col], z_send.at[peer], z_recv.at[col], (peer, bulk))
+
+    def arrived(step):
+        peer = other_col(step)
+        return ring_copy(planes.at[peer], planes.at[peer], z_send.at[peer], z_recv.at[peer], (peer, bulk))
+
+    def spread(step):
+        peer = other_bulk(step)
+        return ring_copy(whole.at[bulk], whole.at[bulk], g_send.at[peer], g_recv.at[bulk], (col, peer))
+
+    def landed(step):
+        peer = other_bulk(step)
+        return ring_copy(whole.at[peer], whole.at[peer], g_send.at[peer], g_recv.at[peer], (col, peer))
+
+    def each(count, what):
+        def body(step, carry):
+            what(step)
+            return carry
+
+        lax.fori_loop(1, count, body, 0)
+
+    each(n_bulk, lambda step: scatter(step).start())
+    parts[bulk] = pack[bulk]
+    each(n_bulk, lambda step: gathered(step).wait_recv())
+    planes[col] = jnp.sum(parts[...], axis=0)
+    each(n_col, lambda step: across(step).start())
+    each(n_col, lambda step: arrived(step).wait_recv())
+    whole[bulk] = jnp.sum(planes[...], axis=0)
+    each(n_bulk, lambda step: spread(step).start())
+    each(n_bulk, lambda step: scatter(step).wait_send())
+    each(n_col, lambda step: across(step).wait_send())
+    each(n_bulk, lambda step: landed(step).wait_recv())
+    for i in range(n_bulk):
+        o_ref[rows * i : rows * (i + 1), :] = whole[i]
+    each(n_bulk, lambda step: spread(step).wait_send())
+
+
+def reduced(x, collective_id):
+    n_col, n_bulk = lax.axis_size("col"), lax.axis_size("bulk")
+    rows = x.shape[0] // n_bulk
+    sems = [pltpu.SemaphoreType.DMA((n_bulk,))] * 2 + [pltpu.SemaphoreType.DMA((n_col,))] * 2
+    return pl.pallas_call(
+        functools.partial(reduce_kernel, n_col, n_bulk, rows),
+        out_shape=jax.ShapeDtypeStruct(x.shape, jnp.float32),
+        in_specs=[pl.BlockSpec(memory_space=pltpu.VMEM)],
+        out_specs=pl.BlockSpec(memory_space=pltpu.VMEM),
+        scratch_shapes=[
+            pltpu.VMEM((n_bulk, rows, 128), jnp.float32),
+            pltpu.VMEM((n_bulk, rows, 128), jnp.float32),
+            pltpu.VMEM((n_col, rows, 128), jnp.float32),
+            pltpu.VMEM((n_bulk, rows, 128), jnp.float32),
+        ]
+        + sems
+        + sems[:2],
+        compiler_params=pltpu.CompilerParams(collective_id=collective_id, has_side_effects=True),
+    )(x)
 
 
 def extended(cells, sides, width):
@@ -140,9 +247,21 @@
     sq_keys = jnp.sum(jnp.square(keys_block.astype(jnp.float32)), axis=1)
     gram_local = jnp.einsum("hiv,hjv->hij", q_heads, k_heads, preferred_element_type=jnp.float32)
     value_local = jnp.einsum("hiv,hjv->hij", g_heads, v_heads, preferred_element_type=jnp.float32)
-    sq_query, sq_keys, gram, value_grad = lax.psum(
-        (sq_query, sq_keys, gram_local, value_local), ("col", "bulk")
-    )
+    first = jnp.concatenate(
+        [
+            gram_local.reshape(channels, head_dim),
+            value_local.reshape(channels, head_dim),
+            sq_query[:, None],
+            sq_keys[:, None],
+            jnp.zeros((channels, 126 - 2 * head_dim), jnp.float32),
+        ],
+        axis=1,
+    )
+    first = reduced(first, 0)
+    gram = first[:, :head_dim].reshape(gram_local.shape)
+    value_grad = first[:, head_dim : 2 * head_dim].reshape(gram_local.shape)
+    sq_query = first[:, 2 * head_dim]
+    sq_keys = first[:, 2 * head_dim + 1]
     inv_query = (1.0 / jnp.sqrt(sq_query + 1e-06)).reshape(group_sequence, head_dim)
     inv_keys = (1.0 / jnp.sqrt(sq_keys + 1e-06)).reshape(group_sequence, head_dim)
     normalized_similarities = gram * inv_query[:, :, None] * inv_keys[:, None, :]
@@ -191,7 +310,12 @@
     source_gradient_part = source_gradient_part.astype(jnp.bfloat16).reshape(
         block_input_field.shape
     )
-    weight_grand_total, depthwise_total = lax.psum((weight_local, depth_local), ("col", "bulk"))
+    second = jnp.concatenate(
+        [weight_local, depth_local, jnp.zeros((3 * channels, 5), jnp.float32)], axis=1
+    )
+    second = reduced(second, 1)
+    weight_grand_total = second[:, :channels]
+    depthwise_total = second[:, channels : channels + 27]
     return (
         source_gradient_part,
         weight_grand_total * multiplier_value,

time: 517 us -> 181 us (0.35)
  waiting for transfers between devices: 250 us -> 6.33 us
  blocking collectives: 159 us -> 0 us
  Pallas kernels: 0 us -> 53.1 us
  local copies, waits for them, and re-layouts: 29.6 us -> 47.7 us
  between operations: 14.8 us -> 1.67 us
  other arithmetic: 36.2 us -> 45 us
    psum x1 -> x0, waiting for transfers between devices: 242 us -> none  [local(): lax.psum((weight_local, depth_local), ('col', 'bulk'))]
    psum x2 -> x0, blocking collectives: 159 us -> none  [the longest x1 83.4 us: local(): lax.psum((sq_query, sq_keys, gram_local, value_local), ('col', 'bulk'))]
    pallas_call x0 -> x2, Pallas kernels: none -> 53.1 us  [reduced(): pl.pallas_call(functools.partial(reduce_kernel, n_col, n_bulk, rows), out...]
    another operation x28 -> x27, local copies, waits for them, and re-layouts: 9.56 us -> 18.5 us  [depth_grad(): return jnp.stack(columns, axis=1)]
  transfers between devices with their start and end apart: 9 -> 8, of which waited for: 5 -> 3; matrix products, arithmetic and copies ran while one was open for 3% -> 17% of each run, Pallas kernels for 0% -> 0%
where the time goes in v1:
time: 181 us; the launch traced here: 180 us
  Pallas kernels  53.1 us (29%)
  local copies, waits for them, and re-layouts  47.7 us (26%)
  other arithmetic  45 us (25%)
  starting transfers between devices  23.7 us (13%)
  waiting for transfers between devices  6.33 us (3%)
  matrix products  2.13 us (1%)
    pallas_call x2, Pallas kernels, reduced(): pl.pallas_call(functools.partial(reduce_kernel, n_col, n_bulk, rows), out...  53.1 us
    another operation x27, local copies, waits for them, and re-layouts, depth_grad(): return jnp.stack(columns, axis=1)  18.5 us
    reduce_sum x3, other arithmetic, depth_grad(): jnp.sum(grads_f * window.astype(jnp.float32), axis=(1, 2, 3))  17 us
    ppermute x4, starting transfers between devices, extended(): lax.ppermute(tail, axis, [(i, (i + 1) % count) for i in range(ends)])  14.5 us
    ppermute x4, starting transfers between devices, extended(): lax.ppermute(head, axis, [((i + 1) % count, i) for i in range(ends)])  9.24 us
    slice x8, local copies, waits for them, and re-layouts, extended(): lax.slice_in_dim(cells, cells.shape[dim] - width, cells.shape[dim], axis=...  8.4 us
    concatenate x6, other arithmetic, extended(): jnp.concatenate([lax.ppermute(tail, axis, [(i, (i + 1) % count) for i in...  8.31 us
    convert_element_type x1, other arithmetic, local(): depth_apply(pad_planes(grad_border), per_channel_kernel, array_shape, True)  5.85 us
  transfers between devices with their start and end apart: 8, of which 3 were waited for; matrix products, arithmetic and copies ran while one was open for 17% of the time, Pallas kernels for 0%

profile of v1, /device:TPU:1, one launch (start us, length us, event | category | flops | bytes accessed | tf_op | source)
XLA Modules:
  0.0 179.6 jit_solution(16044065024674789434)
XLA Ops:
  0.6 1.1 reshape.184
  2.5 1.1 fusion.94
  4.3 4.3 %collective-permute-start = (bf16[288,4,2,1]{0,1,3,2:T(4,128)(2,1)S(1)}, bf16[288,4,2,1]{0,1,3,2:T(4,128)(2,1)S(1)}, u32[]{:S(2)}, u32[]{:S(2)}) collective-permute-start(bf16[288,4,2,1]{0,1,3,2:T(4,128)(2,1)S(1)} %copy.178), channel_id=1, source_target_pairs={{0,32},{32,64},{64,96},{96,128},{128,160},{160,192},{192,224},{1,3... | collective-permute-start | bytes 13832 | tf_op jit(solution)/shard_map/ppermute | solution.py:124
  9.3 1.3 collective-permute-start.1
  11.1 2.8 %collective-permute-done.1 = bf16[288,4,2,1]{0,1,3,2:T(4,128)(2,1)S(1)} collective-permute-done((bf16[288,4,2,1]{0,1,3,2:T(4,128)(2,1)S(1)}, bf16[288,4,2,1]{0,1,3,2:T(4,128)(2,1)S(1)}, u32[]{:S(2)}, u32[]{:S(2)}) %collective-permute-start.1) | collective-permute-done | bytes 4640 | tf_op jit(solution)/shard_map/ppermute | solution.py:126
  15.1 1.1 copy.184
  16.1 3.8 %collective-permute-start.3 = (bf16[288,4,1,130]{0,1,3,2:T(4,128)(2,1)}, bf16[288,4,1,130]{0,1,3,2:T(4,128)(2,1)S(1)}, u32[]{:S(2)}, u32[]{:S(2)}) collective-permute-start(bf16[288,4,1,130]{0,1,3,2:T(4,128)(2,1)} %copy.184), channel_id=1, source_target_pairs={{1,0},{2,1},{3,2},{4,3},{5,4},{6,5},{7,6},{8,7},{9,8},{10,9},{11,1... | collective-permute-start | bytes 898568 | tf_op jit(solution)/shard_map/ppermute | solution.py:126
  20.0 1.1 copy.183
  21.0 3.2 %collective-permute-start.2 = (bf16[288,4,1,130]{0,1,3,2:T(4,128)(2,1)}, bf16[288,4,1,130]{0,1,3,2:T(4,128)(2,1)}, u32[]{:S(2)}, u32[]{:S(2)}) collective-permute-start(bf16[288,4,1,130]{0,1,3,2:T(4,128)(2,1)} %copy.183), channel_id=1, source_target_pairs={{0,1},{1,2},{2,3},{3,4},{4,5},{5,6},{6,7},{7,8},{8,9},{9,10},{10,1... | collective-permute-start | bytes 898568 | tf_op jit(solution)/shard_map/ppermute | solution.py:124
  25.2 1.5 collective-permute-done.3
  27.2 2.0 %collective-permute-done.2 = bf16[288,4,1,130]{0,1,3,2:T(4,128)(2,1)} collective-permute-done((bf16[288,4,1,130]{0,1,3,2:T(4,128)(2,1)}, bf16[288,4,1,130]{0,1,3,2:T(4,128)(2,1)}, u32[]{:S(2)}, u32[]{:S(2)}) %collective-permute-start.2) | collective-permute-done | bytes 299552 | tf_op jit(solution)/shard_map/ppermute | solution.py:124
  29.1 1.3 copy.185
  30.5 1.3 fusion.10
  31.8 2.1 %maximum_maximum_fusion = (bf16[288,4,3,130]{3,0,2,1:T(8,128)(2,1)S(1)}, bf16[288,4,3,130]{3,0,2,1:T(8,128)(2,1)S(1)}) fusion(bf16[288,4,2,1]{3,0,2,1:T(8,128)(2,1)S(1)} %copy.182, bf16[288,4,2,128]{3,0,2,1:T(8,128)(2,1)S(1)} %copy.181, bf16[288,4,2,1]{3,0,2,1:T(8,128)(2,1)S(1)} %copy.180, bf16[288,4,1,130]{3,0,2,1:T(8,128)(2,1)S(1)} %copy.185, ...), kind=kLoop, calls=%fused_computation.46 | loop fusion | flops 7188480 | bytes 2995200 | tf_op jit(solution)/shard_map/concatenate | solution.py:122
  34.0 5.8 %fusion.41 = bf16[288,4,2,128]{3,0,2,1:T(8,128)(2,1)S(1)} fusion(bf16[288,4,2,128]{3,0,2,1:T(8,128)(2,1)S(1)} %copy.181, f32[288]{0:T(512)S(1)} %get-tuple-element.86, f32[288]{0:T(512)S(1)} %get-tuple-element.87, f32[288]{0:T(512)S(1)} %get-tuple-element.62, f32[288]{0:T(512)S(1)} %get-tuple-element.63, f32[288]{0:T(512)S(1)} %get-tuple-element.64, ...), kind=kLoop, calls=%fused_computation.105 | loop fusion | flops 25657344 | bytes 15375744 | tf_op jit(solution)/shard_map/convert_element_type | solution.py:234
  42.4 29.2 %shard_map.84 = f32[96,128]{1,0:T(8,128)} custom-call(f32[96,128]{1,0:T(8,128)} %concatenate.77.x_ref), custom_call_target="tpu_custom_call" | custom-call | tf_op jit(solution)/shard_map/pallas_call | solution.py:99
  71.7 1.1 rsqrt_reduce_fusion.1
  72.9 1.1 fusion.95
  74.0 1.1 multiply_reduce_fusion.6
  75.2 1.1 multiply_reduce_fusion.3
  78.7 10.1 %fusion.81 = (f32[288]{0:T(512)}, f32[288]{0:T(512)}, f32[288]{0:T(512)}, f32[288]{0:T(512)}, f32[288]{0:T(512)}, /*index=5*/f32[288]{0:T(512)}, f32[288]{0:T(51...) fusion(bf16[288,4,2,128]{3,0,2,1:T(8,128)(2,1)S(1)} %copy_dynam, ...), kind=kLoop, calls=%fused_computation.145 | loop fusion | flops 16214976 | bytes 11227392 | tf_op jit(solution)/shard_map/reduce_sum | solution.py:167
  88.7 1.0 fusion.92
  89.8 1.4 copy.207
  91.4 1.3 collective-permute-start.5
  92.7 4.2 %collective-permute-start.4 = (bf16[288,4,2,1]{0,1,3,2:T(4,128)(2,1)S(1)}, bf16[288,4,2,1]{0,1,3,2:T(4,128)(2,1)S(1)}, u32[]{:S(2)}, u32[]{:S(2)}) collective-permute-start(bf16[288,4,2,1]{0,1,3,2:T(4,128)(2,1)S(1)} %copy.207), channel_id=1, source_target_pairs={{0,32},{32,64},{64,96},{96,128},{128,160},{160,192},{192,224},{1,3... | collective-permute-start | bytes 13832 | tf_op jit(solution)/shard_map/ppermute | solution.py:124
  96.9 5.8 %fusion.72 = (f32[288]{0:T(512)S(1)}, f32[288]{0:T(512)}, f32[288]{0:T(512)}, f32[288]{0:T(512)}, f32[288]{0:T(512)}, /*index=5*/f32[288]{0:T(512)}, f32[288]{0:T(512)}, f32[288]{0:T(512)}) fusion(bf16[288,4,2,128]{3,0,2,1:T(8,128)(2,1)S(1)} %copy_dynamic-update-slice_fusion, bf16[288,4,3,130]{3,0,2,1:T(8,128)(2,1)} %copy-done.3, ...), kind=kLoop, calls=%fused_computation.136 | loop fusion | flops 9139968 | bytes 4737024 | tf_op jit(solution)/shard_map/reduce_sum | solution.py:167
  104.1 0.9 fusion.90
  105.0 2.2 %copy.211 = bf16[288,4,1,130]{0,1,3,2:T(4,128)(2,1)} copy(bf16[288,4,1,130]{3,0,2,1:T(8,128)(2,1)} %get-tuple-element.92) | data formatting | bytes 599040 | tf_op jit(solution)/shard_map/slice | solution.py:121
  107.2 1.1 copy.212
  108.3 2.9 %collective-permute-start.7 = (bf16[288,4,1,130]{0,1,3,2:T(4,128)(2,1)}, bf16[288,4,1,130]{0,1,3,2:T(4,128)(2,1)S(1)}, u32[]{:S(2)}, u32[]{:S(2)}) collective-permute-start(bf16[288,4,1,130]{0,1,3,2:T(4,128)(2,1)} %copy.212), channel_id=1, source_target_pairs={{1,0},{2,1},{3,2},{4,3},{5,4},{6,5},{7,6},{8,7},{9,8},{10,9},{11,1... | collective-permute-start | bytes 898568 | tf_op jit(solution)/shard_map/ppermute | solution.py:126
  111.2 2.7 %collective-permute-start.6 = (bf16[288,4,1,130]{0,1,3,2:T(4,128)(2,1)}, bf16[288,4,1,130]{0,1,3,2:T(4,128)(2,1)}, u32[]{:S(2)}, u32[]{:S(2)}) collective-permute-start(bf16[288,4,1,130]{0,1,3,2:T(4,128)(2,1)} %copy.211), channel_id=1, source_target_pairs={{0,1},{1,2},{2,3},{3,4},{4,5},{5,6},{6,7},{7,8},{8,9},{9,10},{10,1... | collective-permute-start | bytes 898568 | tf_op jit(solution)/shard_map/ppermute | solution.py:124
  113.9 1.2 multiply_reduce_fusion
  116.5 0.8 stack.124
  118.0 0.8 stack.117
  121.0 0.8 stack.110
  123.3 0.8 stack.113
  124.9 0.8 stack.115
  132.5 0.8 stack.108
  133.3 0.8 stack.109
  134.9 1.3 copy.213
  136.3 1.3 select_maximum_fusion
  137.6 2.1 %pad_maximum_fusion.1 = (bf16[288,4,3,130]{3,0,2,1:T(8,128)(2,1)S(1)}, bf16[288,4,3,130]{3,0,2,1:T(8,128)(2,1)S(1)}) fusion(bf16[288,4,1,130]{3,0,2,1:T(8,128)(2,1)S(1)} %copy.214, bf16[288,4,2,1]{3,0,2,1:T(8,128)(2,1)S(1)} %copy.210, bf16[288,4,2,128]{3,0,2,1:T(8,128)(2,1)S(1)} %copy_dynamic-update-slice_fusion, bf16[288,4,2,1]{3,0,2,1:T(8,128)(2,1)S(1)} %copy.209, ...), kind=kLoop, calls=%fused_computation.48 | loop fusion | flops 7188480 | bytes 2995200 | tf_op jit(solution)/shard_map/concatenate | solution.py:122
  139.8 5.8 %fusion.82 = bf16[288,4,2,128]{3,0,2,1:T(8,128)(2,1)S(1)} fusion(bf16[288,4,2,128]{3,0,2,1:T(8,128)(2,1)S(1)} %copy_dynamic-update-slice_fusion, bf16[288,6,4,130]{3,0,2,1:T(8,128)(2,1)S(1)} %select_maximum_fusion, bf16[288,4,3,130]{3,0,2,1:T(8,128)(2,1)S(1)} %get-tuple-element.89, bf16[288,4,2,1]{3,0,2,1:T(8,128)(2,1)S(1)} %copy.209, ...), kind=kLoop, calls=%fused_computation.149 | loop fusion | flops 25657344 | bytes 15375744 | tf_op jit(solution)/shard_map/convert_element_type | solution.py:296
  147.2 3.7 %concatenate.92.x_ref = f32[288,128]{1,0:T(8,128)} concatenate(f32[288,96]{1,0:T(8,128)S(1)} %convolution_bitcast_fusion, f32[288,1]{1,0:T(8,128)} %stack.108, f32[288,1]{1,0:T(8,128)} %stack.109, f32[288,1]{1,0:T(8,128)S(1)} %copy-done.15, f32[288,1]{1,0:T(8,128)S(1)} %copy-done.16, f32[288,1]{1,0:T(8,128)S(1)} %copy-done.17, f32[288,1]{1,0:T(8,128)S(1)} %copy-done.18, ...), dimensions={1} | concatenate | bytes 294912 | tf_op jit(solution)/shard_map/concatenate | solution.py:313
  150.9 23.9 %shard_map.85 = f32[288,128]{1,0:T(8,128)} custom-call(f32[288,128]{1,0:T(8,128)} %concatenate.92.x_ref), custom_call_target="tpu_custom_call" | custom-call | tf_op jit(solution)/shard_map/pallas_call | solution.py:99
  174.7 1.0 slice_multiply_fusion
  175.8 1.6 slice_multiply_fusion.1
  178.1 0.8 reshape.195
  (206 shorter events, 29.0 us)
Async XLA Ops:
  4.3 6.5 %collective-permute-start = (bf16[288,4,2,1]{0,1,3,2:T(4,128)(2,1)S(1)}, bf16[288,4,2,1]{0,1,3,2:T(4,128)(2,1)S(1)}, u32[]{:S(2)}, u32[]{:S(2)}) collective-permute-start(bf16[288,4,2,1]{0,1,3,2:T(4,128)(2,1)S(1)} %copy.178), channel_id=1, source_target_pairs={{0,32},{32,64},{64,96},{96,128},{128,160},{160,192},{192,224},{1,3... | collective-permute-start | bytes 13832 | tf_op jit(solution)/shard_map/ppermute | solution.py:124
  9.3 4.6 %collective-permute-start.1 = (bf16[288,4,2,1]{0,1,3,2:T(4,128)(2,1)S(1)}, bf16[288,4,2,1]{0,1,3,2:T(4,128)(2,1)S(1)}, u32[]{:S(2)}, u32[]{:S(2)}) collective-permute-start(bf16[288,4,2,1]{0,1,3,2:T(4,128)(2,1)S(1)} %copy.179), channel_id=1, source_target_pairs={{32,0},{64,32},{96,64},{128,96},{160,128},{192,160},{224,192},{33,... | collective-permute-start | bytes 13832 | tf_op jit(solution)/shard_map/ppermute | solution.py:126
  15.1 9.2 %copy-start.57 = (f32[2]{0:T(128)S(1)}, f32[2]{0:T(128)}, u32[]{:S(2)}) copy-start(f32[2]{0:T(128)} %param.9) | copy-start | bytes 28
  15.1 9.8 %copy-start.19 = (bf16[96,4,2,128]{3,2,1,0:T(2,128)(2,1)S(1)}, bf16[96,4,2,128]{3,2,1,0:T(2,128)(2,1)}, u32[]{:S(2)}) copy-start(bf16[96,4,2,128]{3,2,1,0:T(2,128)(2,1)} %param.6) | copy-start | bytes 589828
  15.1 10.0 %copy-start.20 = (f32[288,27]{0,1:T(8,128)S(1)}, f32[288,27]{0,1:T(8,128)}, u32[]{:S(2)}) copy-start(f32[288,27]{0,1:T(8,128)} %param.8) | copy-start | bytes 93316
  16.1 10.6 %collective-permute-start.3 = (bf16[288,4,1,130]{0,1,3,2:T(4,128)(2,1)}, bf16[288,4,1,130]{0,1,3,2:T(4,128)(2,1)S(1)}, u32[]{:S(2)}, u32[]{:S(2)}) collective-permute-start(bf16[288,4,1,130]{0,1,3,2:T(4,128)(2,1)} %copy.184), channel_id=1, source_target_pairs={{1,0},{2,1},{3,2},{4,3},{5,4},{6,5},{7,6},{8,7},{9,8},{10,9},{11,1... | collective-permute-start | bytes 898568 | tf_op jit(solution)/shard_map/ppermute | solution.py:126
  21.0 8.1 %collective-permute-start.2 = (bf16[288,4,1,130]{0,1,3,2:T(4,128)(2,1)}, bf16[288,4,1,130]{0,1,3,2:T(4,128)(2,1)}, u32[]{:S(2)}, u32[]{:S(2)}) collective-permute-start(bf16[288,4,1,130]{0,1,3,2:T(4,128)(2,1)} %copy.183), channel_id=1, source_target_pairs={{0,1},{1,2},{2,3},{3,4},{4,5},{5,6},{6,7},{7,8},{8,9},{9,10},{10,1... | collective-permute-start | bytes 898568 | tf_op jit(solution)/shard_map/ppermute | solution.py:124
  25.2 8.7 %copy-start.21 = (f32[288]{0:T(512)}, f32[288]{0:T(512)S(1)}, u32[]{:S(2)}) copy-start(f32[288]{0:T(512)S(1)} %get-tuple-element.75) | copy-start | bytes 3460
  25.2 8.8 %copy-start.23 = (f32[288]{0:T(512)}, f32[288]{0:T(512)S(1)}, u32[]{:S(2)}) copy-start(f32[288]{0:T(512)S(1)} %get-tuple-element.76) | copy-start | bytes 3460
  25.2 8.8 %copy-start.25 = (f32[288]{0:T(512)}, f32[288]{0:T(512)S(1)}, u32[]{:S(2)}) copy-start(f32[288]{0:T(512)S(1)} %get-tuple-element.77) | copy-start | bytes 3460
  25.2 8.8 %copy-start.27 = (f32[288]{0:T(512)}, f32[288]{0:T(512)S(1)}, u32[]{:S(2)}) copy-start(f32[288]{0:T(512)S(1)} %get-tuple-element.78) | copy-start | bytes 3460
  25.2 8.8 %copy-start.29 = (f32[288]{0:T(512)}, f32[288]{0:T(512)S(1)}, u32[]{:S(2)}) copy-start(f32[288]{0:T(512)S(1)} %get-tuple-element.79) | copy-start | bytes 3460
  31.8 2.2 %copy-start.1 = (bf16[288,6,4,130]{3,0,2,1:T(8,128)(2,1)}, bf16[288,6,4,130]{3,0,2,1:T(8,128)(2,1)S(1)}, u32[]{:S(2)}) copy-start(bf16[288,6,4,130]{3,0,2,1:T(8,128)(2,1)S(1)} %fusion.10) | copy-start | bytes 5391364
  33.9 5.9 %copy-start.2 = (bf16[288,4,3,130]{3,0,2,1:T(8,128)(2,1)}, bf16[288,4,3,130]{3,0,2,1:T(8,128)(2,1)S(1)}, u32[]{:S(2)}) copy-start(bf16[288,4,3,130]{3,0,2,1:T(8,128)(2,1)S(1)} %get-tuple-element.90) | copy-start | bytes 2695684
  33.9 5.9 %copy-start.3 = (bf16[288,4,3,130]{3,0,2,1:T(8,128)(2,1)}, bf16[288,4,3,130]{3,0,2,1:T(8,128)(2,1)S(1)}, u32[]{:S(2)}) copy-start(bf16[288,4,3,130]{3,0,2,1:T(8,128)(2,1)S(1)} %get-tuple-element.91) | copy-start | bytes 2695684
  41.0 31.9 %copy-start.56 = (f32[96]{0:T(128)S(1)}, f32[96]{0:T(128)}, u32[]{:S(2)}) copy-start(f32[96]{0:T(128)} %mul.756) | copy-start | bytes 1156
  41.2 35.4 %copy-start.58 = (f32[2]{0:T(128)S(1)}, f32[2]{0:T(128)}, u32[]{:S(2)}) copy-start(f32[2]{0:T(128)} %param.9) | copy-start | bytes 28
  91.4 11.6 %collective-permute-start.5 = (bf16[288,4,2,1]{0,1,3,2:T(4,128)(2,1)S(1)}, bf16[288,4,2,1]{0,1,3,2:T(4,128)(2,1)S(1)}, u32[]{:S(2)}, u32[]{:S(2)}) collective-permute-start(bf16[288,4,2,1]{0,1,3,2:T(4,128)(2,1)S(1)} %copy.208), channel_id=1, source_target_pairs={{32,0},{64,32},{96,64},{128,96},{160,128},{192,160},{224,192},{33,... | collective-permute-start | bytes 13832 | tf_op jit(solution)/shard_map/ppermute | solution.py:126
  92.7 10.0 %collective-permute-start.4 = (bf16[288,4,2,1]{0,1,3,2:T(4,128)(2,1)S(1)}, bf16[288,4,2,1]{0,1,3,2:T(4,128)(2,1)S(1)}, u32[]{:S(2)}, u32[]{:S(2)}) collective-permute-start(bf16[288,4,2,1]{0,1,3,2:T(4,128)(2,1)S(1)} %copy.207), channel_id=1, source_target_pairs={{0,32},{32,64},{64,96},{96,128},{128,160},{160,192},{192,224},{1,3... | collective-permute-start | bytes 13832 | tf_op jit(solution)/shard_map/ppermute | solution.py:124
  105.0 8.9 %copy-start.5 = (bf16[288,1024]{1,0:T(8,128)(2,1)S(1)}, bf16[288,1024]{1,0:T(8,128)(2,1)}, u32[]{:S(2)}) copy-start(bf16[288,1024]{1,0:T(8,128)(2,1)} %copy-done.4) | copy-start | bytes 1769476
  108.3 7.3 %copy-start.48 = (f32[288]{0:T(512)S(1)}, f32[288]{0:T(512)}, u32[]{:S(2)}) copy-start(f32[288]{0:T(512)} %get-tuple-element.24) | copy-start | bytes 3460
  108.3 7.4 %copy-start.55 = (f32[288]{0:T(512)S(1)}, f32[288]{0:T(512)}, u32[]{:S(2)}) copy-start(f32[288]{0:T(512)} %get-tuple-element.43) | copy-start | bytes 3460
  108.3 8.2 %copy-start.54 = (f32[288]{0:T(512)S(1)}, f32[288]{0:T(512)}, u32[]{:S(2)}) copy-start(f32[288]{0:T(512)} %get-tuple-element.44) | copy-start | bytes 3460
  108.3 8.9 %copy-start.53 = (f32[288]{0:T(512)S(1)}, f32[288]{0:T(512)}, u32[]{:S(2)}) copy-start(f32[288]{0:T(512)} %get-tuple-element.50) | copy-start | bytes 3460
  108.3 9.7 %copy-start.52 = (f32[288]{0:T(512)S(1)}, f32[288]{0:T(512)}, u32[]{:S(2)}) copy-start(f32[288]{0:T(512)} %get-tuple-element.51) | copy-start | bytes 3460
  108.3 10.5 %copy-start.51 = (f32[288]{0:T(512)S(1)}, f32[288]{0:T(512)}, u32[]{:S(2)}) copy-start(f32[288]{0:T(512)} %get-tuple-element.52) | copy-start | bytes 3460
  108.3 26.2 %collective-permute-start.7 = (bf16[288,4,1,130]{0,1,3,2:T(4,128)(2,1)}, bf16[288,4,1,130]{0,1,3,2:T(4,128)(2,1)S(1)}, u32[]{:S(2)}, u32[]{:S(2)}) collective-permute-start(bf16[288,4,1,130]{0,1,3,2:T(4,128)(2,1)} %copy.212), channel_id=1, source_target_pairs={{1,0},{2,1},{3,2},{4,3},{5,4},{6,5},{7,6},{8,7},{9,8},{10,9},{11,1... | collective-permute-start | bytes 898568 | tf_op jit(solution)/shard_map/ppermute | solution.py:126
  111.2 23.8 %collective-permute-start.6 = (bf16[288,4,1,130]{0,1,3,2:T(4,128)(2,1)}, bf16[288,4,1,130]{0,1,3,2:T(4,128)(2,1)}, u32[]{:S(2)}, u32[]{:S(2)}) collective-permute-start(bf16[288,4,1,130]{0,1,3,2:T(4,128)(2,1)} %copy.211), channel_id=1, source_target_pairs={{0,1},{1,2},{2,3},{3,4},{4,5},{5,6},{6,7},{7,8},{8,9},{9,10},{10,1... | collective-permute-start | bytes 898568 | tf_op jit(solution)/shard_map/ppermute | solution.py:124
  113.9 5.6 %copy-start.50 = (f32[288]{0:T(512)S(1)}, f32[288]{0:T(512)}, u32[]{:S(2)}) copy-start(f32[288]{0:T(512)} %get-tuple-element.53) | copy-start | bytes 3460
  113.9 6.4 %copy-start.49 = (f32[288]{0:T(512)S(1)}, f32[288]{0:T(512)}, u32[]{:S(2)}) copy-start(f32[288]{0:T(512)} %get-tuple-element.54) | copy-start | bytes 3460
  113.9 7.1 %copy-start.47 = (f32[288]{0:T(512)S(1)}, f32[288]{0:T(512)}, u32[]{:S(2)}) copy-start(f32[288]{0:T(512)} %get-tuple-element.25) | copy-start | bytes 3460
  113.9 7.9 %copy-start.46 = (f32[288]{0:T(512)S(1)}, f32[288]{0:T(512)}, u32[]{:S(2)}) copy-start(f32[288]{0:T(512)} %get-tuple-element.26) | copy-start | bytes 3460
  115.1 7.5 %copy-start.45 = (f32[288]{0:T(512)S(1)}, f32[288]{0:T(512)}, u32[]{:S(2)}) copy-start(f32[288]{0:T(512)} %get-tuple-element.27) | copy-start | bytes 3460
  115.1 8.2 %copy-start.44 = (f32[288]{0:T(512)S(1)}, f32[288]{0:T(512)}, u32[]{:S(2)}) copy-start(f32[288]{0:T(512)} %get-tuple-element.28) | copy-start | bytes 3460
  115.1 9.0 %copy-start.43 = (f32[288]{0:T(512)S(1)}, f32[288]{0:T(512)}, u32[]{:S(2)}) copy-start(f32[288]{0:T(512)} %get-tuple-element.29) | copy-start | bytes 3460
  115.1 9.7 %copy-start.42 = (f32[288]{0:T(512)S(1)}, f32[288]{0:T(512)}, u32[]{:S(2)}) copy-start(f32[288]{0:T(512)} %get-tuple-element.30) | copy-start | bytes 3460
  115.3 10.3 %copy-start.41 = (f32[288]{0:T(512)S(1)}, f32[288]{0:T(512)}, u32[]{:S(2)}) copy-start(f32[288]{0:T(512)} %get-tuple-element.31) | copy-start | bytes 3460
  115.5 10.9 %copy-start.40 = (f32[288]{0:T(512)S(1)}, f32[288]{0:T(512)}, u32[]{:S(2)}) copy-start(f32[288]{0:T(512)} %get-tuple-element.32) | copy-start | bytes 3460
  115.6 11.6 %copy-start.39 = (f32[288]{0:T(512)S(1)}, f32[288]{0:T(512)}, u32[]{:S(2)}) copy-start(f32[288]{0:T(512)} %get-tuple-element.33) | copy-start | bytes 3460
  115.7 12.2 %copy-start.38 = (f32[288]{0:T(512)S(1)}, f32[288]{0:T(512)}, u32[]{:S(2)}) copy-start(f32[288]{0:T(512)} %get-tuple-element.34) | copy-start | bytes 3460
  116.5 12.2 %copy-start.37 = (f32[288]{0:T(512)S(1)}, f32[288]{0:T(512)}, u32[]{:S(2)}) copy-start(f32[288]{0:T(512)} %get-tuple-element.35) | copy-start | bytes 3460
  117.2 12.2 %copy-start.36 = (f32[288]{0:T(512)S(1)}, f32[288]{0:T(512)}, u32[]{:S(2)}) copy-start(f32[288]{0:T(512)} %get-tuple-element.36) | copy-start | bytes 3460
  118.0 12.2 %copy-start.35 = (f32[288]{0:T(512)S(1)}, f32[288]{0:T(512)}, u32[]{:S(2)}) copy-start(f32[288]{0:T(512)} %get-tuple-element.37) | copy-start | bytes 3460
  118.8 12.2 %copy-start.34 = (f32[288]{0:T(512)S(1)}, f32[288]{0:T(512)}, u32[]{:S(2)}) copy-start(f32[288]{0:T(512)} %get-tuple-element.38) | copy-start | bytes 3460
  119.5 12.2 %copy-start.33 = (f32[288]{0:T(512)S(1)}, f32[288]{0:T(512)}, u32[]{:S(2)}) copy-start(f32[288]{0:T(512)} %get-tuple-element.39) | copy-start | bytes 3460
  120.3 12.2 %copy-start.32 = (f32[288]{0:T(512)S(1)}, f32[288]{0:T(512)}, u32[]{:S(2)}) copy-start(f32[288]{0:T(512)} %get-tuple-element.40) | copy-start | bytes 3460
  121.0 12.2 %copy-start.31 = (f32[288]{0:T(512)S(1)}, f32[288]{0:T(512)}, u32[]{:S(2)}) copy-start(f32[288]{0:T(512)} %get-tuple-element.41) | copy-start | bytes 3460
  139.8 5.9 %copy-start.6 = (bf16[96,4,2,128]{3,2,1,0:T(2,128)(2,1)S(1)}, bf16[96,4,2,128]{3,2,1,0:T(2,128)(2,1)}, u32[]{:S(2)}) copy-start(bf16[96,4,2,128]{3,2,1,0:T(2,128)(2,1)} %param.5) | copy-start | bytes 589828
  (19 other events, 27.2 us)

commit v2 on v0

v2 whole, which is shorter than its diff:
```python
import functools
import math

import jax
import jax.numpy as jnp
import numpy as np
from jax import lax
from jax.experimental import pallas as pl
from jax.experimental.pallas import tpu as pltpu
from jax.sharding import PartitionSpec as P

MESH = pl.DeviceIdType.MESH
F32 = jnp.float32
BF16 = jnp.bfloat16
C = 96
HEAD = 48
C3 = 3 * C
LANES = 128
CHUNK = 32
EDGE_COLUMNS = (0, 1, LANES - 2, LANES - 1)
NEIGHBOURS = [(a, b) for a in (-1, 0, 1) for b in (-1, 0, 1)]


def slot_of(a, b):
    return 3 * (a + 1) + b + 1


def edge_index(z, y):
    return (z + 1) * 6 + y + 2


def edge_tables():
    place = np.zeros((3, LANES, 9 * 32), np.float32)
    flags = np.zeros((8, LANES), np.float32)
    for (a, b) in NEIGHBOURS:
        for s, column in enumerate(EDGE_COLUMNS):
            x = LANES * a + column
            for y in range(2):
                for z in range(4):
                    k = slot_of(a, b) * 32 + s * 8 + y * 4 + z
                    index = 2 * edge_index(z, 2 * b + y)
                    for c in (-1, 0, 1):
                        if x == -1 + c:
                            place[c + 1, index + 1, k] = 1.0
                        if x == LANES + c:
                            place[c + 1, index, k] = 1.0
    for z in range(4):
        for y in range(-1, 3):
            for left in range(2):
                lane = 2 * edge_index(z, y) + left
                flags[0, lane] = 1.0
                flags[1, lane] = left
                flags[2, lane] = 1 - left
                flags[3, lane] = y == -1
                flags[4, lane] = y == 2
    return place.reshape(3 * LANES, 9 * 32), flags


def dot_nt(a, b):
    return lax.dot_general(a, b, (((1,), (1,)), ((), ())), preferred_element_type=F32)


def dot_tn(a, b):
    return lax.dot_general(a, b, (((0,), (0,)), ((), ())), preferred_element_type=F32)


def dot(a, b):
    return jnp.dot(a, b, preferred_element_type=F32)


def iota(shape, dim):
    return lax.broadcasted_iota(jnp.int32, shape, dim)


def rounded(v):
    return v.astype(BF16).astype(F32)


def remote(src, dst, send, recv, target):
    return pltpu.make_async_remote_copy(
        src_ref=src, dst_ref=dst, send_sem=send, recv_sem=recv, device_id=target, device_id_type=MESH
    )


def each(count, what):
    def body(step, carry):
        what(step)
        return carry

    lax.fori_loop(1, count, body, 0)


class Reduction:
    def __init__(self, sizes, place, pack, parts, planes, whole, sems):
        self.n_col, self.n_bulk = sizes
        self.col, self.bulk = place
        self.pack, self.parts, self.planes, self.whole = pack, parts, planes, whole
        self.s_send, self.s_recv, self.z_send, self.z_recv, self.g_send, self.g_recv = sems

    def bulk_peer(self, step):
        return lax.rem(self.bulk + step, self.n_bulk)

    def col_peer(self, step):
        return lax.rem(self.col + step, self.n_col)

    def scatter(self, step, incoming=False):
        peer = self.bulk_peer(step)
        slot = peer if incoming else self.bulk
        return remote(
            self.pack.at[peer], self.parts.at[slot], self.s_send.at[peer], self.s_recv.at[slot], (self.col, peer)
        )

    def across(self, step, incoming=False):
        peer = self.col_peer(step)
        slot = peer if incoming else self.col
        return remote(
            self.planes.at[slot], self.planes.at[slot], self.z_send.at[peer], self.z_recv.at[slot], (peer, self.bulk)
        )

    def spread(self, step, incoming=False):
        peer = self.bulk_peer(step)
        slot = peer if incoming else self.bulk
        return remote(
            self.whole.at[slot], self.whole.at[slot], self.g_send.at[peer], self.g_recv.at[slot], (self.col, peer)
        )

    def start(self):
        each(self.n_bulk, lambda step: self.scatter(step).start())
        self.parts[self.bulk] = self.pack[self.bulk]

    def middle(self):
        each(self.n_bulk, lambda step: self.scatter(step, True).wait_recv())
        self.planes[self.col] = jnp.sum(self.parts[...], axis=0)
        each(self.n_col, lambda step: self.across(step).start())

    def final(self):
        each(self.n_col, lambda step: self.across(step, True).wait_recv())
        self.whole[self.bulk] = jnp.sum(self.planes[...], axis=0)
        each(self.n_bulk, lambda step: self.spread(step).start())

    def finish(self):
        each(self.n_bulk, lambda step: self.spread(step, True).wait_recv())

    def drain(self):
        each(self.n_bulk, lambda step: self.scatter(step).wait_send())
        each(self.n_col, lambda step: self.across(step).wait_send())
        each(self.n_bulk, lambda step: self.spread(step).wait_send())


def conv(source, y0, weights, flip, sink):
    def body(j, carry):
        rows = pl.ds(pl.multiple_of(j * CHUNK, CHUNK), CHUNK)
        total = [None] * 4
        for b in range(3):
            for c in range(3):
                cells = [source[c, y0 + b, z, rows, :] for z in range(4)]
                for a in range(3):
                    tap = 9 * a + 3 * b + c
                    weight = weights[26 - tap if flip else tap, rows, :]
                    for z in range(4):
                        if 0 <= z + a - 1 < 4:
                            term = weight * cells[z + a - 1]
                            total[z] = term if total[z] is None else total[z] + term
        for z in range(4):
            sink(z, rows, total[z])
        return carry

    lax.fori_loop(0, C3 // CHUNK, body, 0)


def kernel(
    sizes,
    scale,
    x_ref,
    g_ref,
    w_ref,
    k_ref,
    sharp_ref,
    place_ref,
    flags_ref,
    dx_ref,
    pd_ref,
    kd_ref,
    sd_ref,
    xh,
    gh,
    messages,
    arrived,
    edge_t,
    edge_x,
    edge_g,
    taps_t,
    taps_c,
    weights,
    field,
    field_edge,
    mixed,
    mixed_edge,
    grads,
    grads_edge,
    field_grad,
    turn,
    couple,
    coef,
    pay1,
    pay2,
    pack1,
    parts1,
    planes1,
    whole1,
    pack2,
    parts2,
    planes2,
    whole2,
    row_send,
    row_recv,
    edge_send,
    edge_recv,
    *sems,
):
    n_col, n_bulk = sizes
    col, bulk = lax.axis_index("col"), lax.axis_index("bulk")
    first = Reduction(sizes, (col, bulk), pack1, parts1, planes1, whole1, sems[:6])
    second = Reduction(sizes, (col, bulk), pack2, parts2, planes2, whole2, sems[6:])
    low, high = bulk > 0, bulk < n_bulk - 1

    xh[...] = jnp.zeros_like(xh)
    gh[...] = jnp.zeros_like(gh)
    arrived[...] = jnp.zeros_like(arrived)
    barrier = pltpu.get_barrier_semaphore()

    def greet(target):
        pl.semaphore_signal(barrier, inc=1, device_id=target, device_id_type=MESH)

    each(n_bulk, lambda step: greet((col, lax.rem(bulk + step, n_bulk))))
    each(n_col, lambda step: greet((lax.rem(col + step, n_col), bulk)))
    for a in (1, n_col - 1):
        for b in (1, n_bulk - 1):
            greet((lax.rem(col + a, n_col), lax.rem(bulk + b, n_bulk)))

    row32, lane32 = iota((32, LANES), 0), iota((32, LANES), 1)
    for k, source in enumerate((x_ref, g_ref)):
        total = jnp.zeros((32, C), F32)
        for y in range(2):
            for z in range(4):
                pick = jnp.zeros((32, LANES), jnp.bool_)
                for s, column in enumerate(EDGE_COLUMNS):
                    pick = pick | ((row32 == s * 8 + y * 4 + z) & (lane32 == column))
                total = total + dot_nt(jnp.where(pick, 1.0, 0.0).astype(BF16), source[y, z])
        messages[k] = jnp.zeros((32, LANES), BF16)
        messages[k, :, 0:C] = total.astype(BF16)

    taps_t[...] = jnp.zeros_like(taps_t)
    taps_t[0:27, 0:C3] = k_ref[...]
    for j in range(3):
        taps_c[LANES * j : LANES * (j + 1), :] = taps_t[:, LANES * j : LANES * (j + 1)].T
    for t in range(27):
        weights[t] = jnp.broadcast_to(taps_c[0:C3, t : t + 1], (C3, LANES))

    pl.semaphore_wait(barrier, n_bulk + n_col - 2 + 4)

    def row_copy(k, down):
        y = 1 if down == (k != 1) else 0
        if k == 2:
            source, target = g_ref.at[y], gh.at[0 if down else 1]
        else:
            source, target = x_ref.at[y], xh.at[(1, 0)[k] if down else (2, 3)[k]]
        sem = 2 * k + (1 if down else 0)
        return remote(source, target, row_send.at[sem], row_recv.at[sem], (col, lax.rem(bulk + (1 if down else n_bulk - 1), n_bulk)))

    def edge_copy(a, b):
        slot = slot_of(-a, -b)
        target = (lax.rem(col + a + n_col, n_col), lax.rem(bulk + b + n_bulk, n_bulk))
        return remote(messages, arrived.at[slot], edge_send.at[slot], edge_recv.at[slot], target)

    def inside(a, b):
        return (col + a >= 0) & (col + a < n_col) & (bulk + b >= 0) & (bulk + b < n_bulk)

    for (a, b) in NEIGHBOURS:
        if (a, b) != (0, 0):
            pl.when(inside(a, b))(lambda a=a, b=b: edge_copy(a, b).start())
    for k in range(3):
        pl.when(high)(lambda k=k: row_copy(k, True).start())
        pl.when(low)(lambda k=k: row_copy(k, False).start())
    arrived[slot_of(0, 0)] = messages[...]

    def wait_row(k):
        pl.when(low)(lambda: row_copy(k, True).wait_recv())
        pl.when(high)(lambda: row_copy(k, False).wait_recv())

    for (a, b) in NEIGHBOURS:
        if (a, b) != (0, 0):
            pl.when(inside(a, b))(lambda a=a, b=b: edge_copy(-a, -b).wait_recv())

    for c in range(3):
        edge_t[c] = dot(
            place_ref[LANES * c : LANES * (c + 1), :], arrived[:, 0].reshape(9 * 32, LANES)
        ).astype(BF16)
    edge_t[3] = dot(place_ref[LANES : 2 * LANES, :], arrived[:, 1].reshape(9 * 32, LANES)).astype(BF16)
    eye = jnp.where(iota((LANES, LANES), 0) == iota((LANES, LANES), 1), 1.0, 0.0).astype(BF16)
    edge_x[...] = dot_nt(eye, edge_t[1])
    edge_g[...] = dot_nt(eye, edge_t[3]).astype(BF16)
    for c in range(3):
        field_edge[c] = rounded(dot_nt(w_ref[...], edge_t[c, :, 0:C]))

    def turned(values, z, y):
        return pltpu.roll(values, LANES - 13 - 2 * (y + 2) - 12 * z, 1)

    def shifted(values, edge):
        lane = iota(values.shape, 1)
        before = jnp.where(lane == 0, edge, pltpu.roll(values, 1, 1))
        after = jnp.where(lane == LANES - 1, edge, pltpu.roll(values, LANES - 1, 1))
        return before, after

    def input_row(y):
        return x_ref.at[y] if y in (0, 1) else xh.at[{-2: 0, -1: 1, 2: 2, 3: 3}[y]]

    def make_field(ys):
        def body(z, carry):
            for y in ys:
                plane = input_row(y)[z]
                before, after = shifted(plane.astype(F32), turned(edge_x[0:C, :], z, y))
                cells = jnp.concatenate([before.astype(BF16), plane, after.astype(BF16)], axis=1)
                made = rounded(dot(w_ref[...], cells))
                for c in range(3):
                    field[c, y + 2, z] = made[:, LANES * c : LANES * (c + 1)]
            return carry

        lax.fori_loop(0, 4, body, 0)

    def make_mixed(y):
        def sink(z, rows, value):
            mixed[y + 1, z, rows, :] = value.astype(BF16)

        conv(field, y + 1, weights, False, sink)

    make_field((0, 1))
    wait_row(0)
    make_field((-1, 2))
    make_mixed(0)
    make_mixed(1)

    row, lane = iota((C, LANES), 0), iota((C, LANES), 1)
    upper = row < HEAD
    gram = jnp.zeros((C, LANES), F32)
    value = jnp.zeros((C, LANES), F32)
    square_q = jnp.zeros((C, LANES), F32)
    square_k = jnp.zeros((C, LANES), F32)
    for y in range(2):
        for z in range(4):
            q, k = mixed[y + 1, z, 0:C, :], mixed[y + 1, z, C : 2 * C, :]
            gram = gram + dot_nt(q, mixed[y + 1, z, C : C + LANES, :])
            value = value + dot_nt(g_ref[y, z], mixed[y + 1, z, C3 - LANES : C3, :])
            square_q = square_q + jnp.square(q.astype(F32))
            square_k = square_k + jnp.square(k.astype(F32))
    gram = jnp.where(upper, gram, pltpu.roll(gram, LANES - HEAD, 1))
    value = jnp.where(upper, pltpu.roll(value, 16, 1), pltpu.roll(value, LANES - 32, 1))
    sum_q = jnp.sum(square_q, axis=1, keepdims=True)
    sum_k = jnp.sum(square_k, axis=1, keepdims=True)
    pay1[...] = jnp.where(
        lane < HEAD,
        gram,
        jnp.where(lane < 2 * HEAD, value, jnp.where(lane == C, sum_q, jnp.where(lane == C + 1, sum_k, 0.0))),
    )
    rows1 = C // n_bulk
    for i in range(n_bulk):
        pack1[i] = pay1[rows1 * i : rows1 * (i + 1), :]
    first.start()

    wait_row(1)
    make_field((-2, 3))
    spread_edge = []
    for a in range(3):
        for b in range(3):
            part = None
            for c in range(3):
                term = weights[9 * a + 3 * b + c] * field_edge[c]
                part = term if part is None else part + term
            step = 12 * (a - 1) + 2 * (b - 1)
            spread_edge.append(pltpu.roll(part, (LANES - step) % LANES, 1))
    mixed_edge[...] = sum(spread_edge[1:], spread_edge[0]).astype(BF16)
    make_mixed(-1)
    first.middle()
    make_mixed(2)
    wait_row(2)
    first.final()
    first.finish()

    for i in range(n_bulk):
        pay1[rows1 * i : rows1 * (i + 1), :] = whole1[i]
    sums = pay1[...]
    value = pltpu.roll(sums, LANES - HEAD, 1)
    inv_q = 1.0 / jnp.sqrt(sums[:, C : C + 1] + 1e-06)
    inv_k = 1.0 / jnp.sqrt(sums[:, C + 1 : C + 2] + 1e-06)
    inv_k0 = jnp.sum(jnp.where(row == lane, inv_k, 0.0), axis=0, keepdims=True)
    inv_k1 = jnp.sum(jnp.where(row == lane + HEAD, inv_k, 0.0), axis=0, keepdims=True)
    inv_kr = jnp.where(upper, inv_k0, inv_k1)
    inner = lane < HEAD
    sharp = jnp.where(upper, sharp_ref[0], sharp_ref[1])
    cosine = jnp.where(inner, sums * inv_q * inv_kr, 0.0)
    numerators = jnp.where(inner, jnp.exp(sharp * cosine), 0.0)
    attention = numerators / jnp.sum(numerators, axis=1, keepdims=True)
    score = attention * (value - jnp.sum(attention * value, axis=1, keepdims=True))
    by_cosine = score * cosine
    sd_ref[0] = jnp.sum(jnp.where(upper, by_cosine, 0.0)) * scale
    sd_ref[1] = jnp.sum(jnp.where(upper, 0.0, by_cosine)) * scale
    cosine_grad = sharp * score
    diagonal = cosine_grad * cosine
    diag_q = jnp.sum(diagonal, axis=1, keepdims=True)
    coupling = rounded(inv_q * cosine_grad * inv_kr)

    def blocks(v):
        return jnp.where(
            upper, jnp.where(inner, v, 0.0), jnp.where((lane >= HEAD) & (lane < C), pltpu.roll(v, HEAD, 1), 0.0)
        )

    def transposed(v):
        turn[0:C, :] = v
        turn[C:LANES, :] = jnp.zeros((LANES - C, LANES), F32)
        return turn[...].T

    coupled = blocks(coupling)
    couple[0] = coupled.astype(BF16)
    couple[1] = transposed(coupled)[0:C, :].astype(BF16)
    couple[2] = transposed(blocks(attention))[0:C, :].astype(BF16)
    diag_k = jnp.sum(transposed(blocks(diagonal)), axis=1, keepdims=True)[0:C, :]
    coef[0] = jnp.broadcast_to(inv_q * inv_q * diag_q, (C, LANES))
    coef[1] = jnp.broadcast_to(inv_k * inv_k * diag_k, (C, LANES))

    def gradients(q, k, g):
        grad_q = dot(couple[0, :, 0:C], k) - coef[0] * q.astype(F32)
        grad_k = dot(couple[1, :, 0:C], q) - coef[1] * k.astype(F32)
        return grad_q, grad_k, dot(couple[2, :, 0:C], g)

    def flag(condition):
        return jnp.where(condition, 1.0, 0.0)

    mask = (
        flags_ref[0:1, :]
        * (1.0 - flags_ref[1:2, :] * flag(col == 0))
        * (1.0 - flags_ref[2:3, :] * flag(col == n_col - 1))
        * (1.0 - flags_ref[3:4, :] * flag(bulk == 0))
        * (1.0 - flags_ref[4:5, :] * flag(bulk == n_bulk - 1))
    )
    edges = gradients(mixed_edge[0:C, :], mixed_edge[C : 2 * C, :], edge_g[0:C, :])
    for part in range(3):
        grads_edge[C * part : C * (part + 1), :] = jnp.where(mask > 0.5, rounded(edges[part]), 0.0)

    def grad_planes(z, carry):
        for y in range(-1, 3):
            g = g_ref[y, z] if y in (0, 1) else gh[0 if y == -1 else 1, z]
            made = gradients(mixed[y + 1, z, 0:C, :], mixed[y + 1, z, C : 2 * C, :], g)
            for part in range(3):
                rows = slice(C * part, C * (part + 1))
                plane = rounded(made[part])
                if y == -1:
                    plane = plane * flag(low)
                if y == 2:
                    plane = plane * flag(high)
                before, after = shifted(plane, turned(grads_edge[rows, :], z, y))
                grads[0, y + 1, z, rows, :] = before
                grads[1, y + 1, z, rows, :] = plane
                grads[2, y + 1, z, rows, :] = after
        return carry

    lax.fori_loop(0, 4, grad_planes, 0)

    for y in range(2):

        def sink(z, rows, value, y=y):
            field_grad[y, z, rows, :] = value.astype(BF16)

        conv(grads, y, weights, True, sink)

    weight = jnp.zeros((C3, C), F32)
    for y in range(2):
        for z in range(4):
            weight = weight + dot_nt(field_grad[y, z], x_ref[y, z])
    pay2[:, 0:C] = weight

    def depth(j, carry):
        rows = pl.ds(pl.multiple_of(j * CHUNK, CHUNK), CHUNK)
        lane = iota((CHUNK, LANES), 1)
        made = pay2[rows, :]
        for b in range(3):
            for c in range(3):
                for a in range(3):
                    total = None
                    for y in range(2):
                        for z in range(4):
                            if 0 <= z + a - 1 < 4:
                                term = grads[1, y + 1, z, rows, :] * field[c, y + b + 1, z + a - 1, rows, :]
                                total = term if total is None else total + term
                    tap = 9 * a + 3 * b + c
                    made = jnp.where(lane == C + tap, jnp.sum(total, axis=1, keepdims=True), made)
        pay2[rows, :] = jnp.where(lane < C + 27, made, 0.0)
        return carry

    lax.fori_loop(0, C3 // CHUNK, depth, 0)
    rows2 = C3 // n_bulk
    for i in range(n_bulk):
        pack2[i] = pay2[rows2 * i : rows2 * (i + 1), :]
    second.start()

    for y in range(2):
        for z in range(4):
            dx_ref[y, z] = dot_tn(w_ref[...], field_grad[y, z]).astype(BF16)
    for k in range(3):
        pl.when(high)(lambda k=k: row_copy(k, True).wait_send())
        pl.when(low)(lambda k=k: row_copy(k, False).wait_send())
    for (a, b) in NEIGHBOURS:
        if (a, b) != (0, 0):
            pl.when(inside(a, b))(lambda a=a, b=b: edge_copy(a, b).wait_send())
    first.drain()
    second.middle()
    second.final()
    second.finish()
    for i in range(n_bulk):
        pay2[rows2 * i : rows2 * (i + 1), :] = whole2[i]
    pd_ref[...] = pay2[:, 0:C] * scale
    kd_ref[...] = pay2[:, C : C + 27] * scale
    second.drain()


def local(x, g, w, k, sharp):
    n_col, n_bulk = lax.axis_size("col"), lax.axis_size("bulk")
    scale = 1.0 / math.sqrt(x.shape[1] * x.shape[2] * x.shape[3] * n_col * n_bulk)
    place, flags = edge_tables()
    vmem = pl.BlockSpec(memory_space=pltpu.VMEM)
    smem = pl.BlockSpec(memory_space=pltpu.SMEM)
    rows1, rows2 = C // n_bulk, C3 // n_bulk

    def reduction(rows):
        return [
            pltpu.VMEM((n_bulk, rows, LANES), F32),
            pltpu.VMEM((n_bulk, rows, LANES), F32),
            pltpu.VMEM((n_col, rows, LANES), F32),
            pltpu.VMEM((n_bulk, rows, LANES), F32),
        ]

    def dma(count):
        return pltpu.SemaphoreType.DMA((count,))

    reduction_sems = [dma(n_bulk), dma(n_bulk), dma(n_col), dma(n_col), dma(n_bulk), dma(n_bulk)]
    dx, pd, kd, sd = pl.pallas_call(
        functools.partial(kernel, (n_col, n_bulk), scale),
        out_shape=(
            jax.ShapeDtypeStruct((2, 4, C, LANES), BF16),
            jax.ShapeDtypeStruct((C3, C), F32),
            jax.ShapeDtypeStruct((C3, 27), F32),
            jax.ShapeDtypeStruct((2,), F32),
        ),
        in_specs=[vmem, vmem, vmem, vmem, smem, vmem, vmem],
        out_specs=(vmem, vmem, vmem, smem),
        scratch_shapes=[
            pltpu.VMEM((4, 4, C, LANES), BF16),
            pltpu.VMEM((2, 4, C, LANES), BF16),
            pltpu.VMEM((2, 32, LANES), BF16),
            pltpu.VMEM((9, 2, 32, LANES), BF16),
            pltpu.VMEM((4, LANES, LANES), BF16),
            pltpu.VMEM((LANES, LANES), F32),
            pltpu.VMEM((LANES, LANES), BF16),
            pltpu.VMEM((LANES, 3 * LANES), F32),
            pltpu.VMEM((3 * LANES, LANES), F32),
            pltpu.VMEM((27, C3, LANES), F32),
            pltpu.VMEM((3, 6, 4, C3, LANES), F32),
            pltpu.VMEM((3, C3, LANES), F32),
            pltpu.VMEM((4, 4, C3, LANES), BF16),
            pltpu.VMEM((C3, LANES), BF16),
            pltpu.VMEM((3, 4, 4, C3, LANES), F32),
            pltpu.VMEM((C3, LANES), F32),
            pltpu.VMEM((2, 4, C3, LANES), BF16),
            pltpu.VMEM((LANES, LANES), F32),
            pltpu.VMEM((3, C, LANES), BF16),
            pltpu.VMEM((2, C, LANES), F32),
            pltpu.VMEM((C, LANES), F32),
            pltpu.VMEM((C3, LANES), F32),
        ]
        + reduction(rows1)
        + reduction(rows2)
        + [dma(6), dma(6), dma(9), dma(9)]
        + reduction_sems
        + reduction_sems,
        compiler_params=pltpu.CompilerParams(
            collective_id=0, has_side_effects=True, vmem_limit_bytes=56 * 2**20
        ),
    )(
        jnp.transpose(x, (2, 1, 0, 3)),
        jnp.transpose(g, (2, 1, 0, 3)),
        w,
        k.T,
        sharp,
        jnp.asarray(place, BF16),
        jnp.asarray(flags),
    )
    return jnp.transpose(dx, (2, 1, 0, 3)), pd, kd, sd


def solution(mesh):
    return jax.shard_map(
        local,
        mesh=mesh,
        in_specs=(P(None, None, "bulk", "col"), P(None, None, "bulk", "col"), P(), P(), P()),
        out_specs=(P(None, None, "bulk", "col"), P(), P(), P()),
        check_vma=False,
    )
```

time: 517 us -> 69.6 us (0.13)
  waiting for transfers between devices: 250 us -> 0 us
  blocking collectives: 159 us -> 0 us
  Pallas kernels: 0 us -> 63.1 us
  other arithmetic: 36.2 us -> 0 us
  starting transfers between devices: 23.9 us -> 0 us
  local copies, waits for them, and re-layouts: 29.6 us -> 5.75 us
  between operations: 14.8 us -> 0.65 us
    psum x1 -> x0, waiting for transfers between devices: 242 us -> none  [local(): lax.psum((weight_local, depth_local), ('col', 'bulk'))]
    psum x2 -> x0, blocking collectives: 159 us -> none  [the longest x1 83.4 us: local(): lax.psum((sq_query, sq_keys, gram_local, value_local), ('col', 'bulk'))]
    pallas_call x0 -> x1, Pallas kernels: none -> 63.1 us  [local(): pl.pallas_call(functools.partial(kernel, (n_col, n_bulk), scale), out_sha...]
    ppermute x8 -> x0, starting transfers between devices: 23.9 us -> none  [the longest x4 13.3 us: extended(): lax.ppermute(tail, axis, [(i, (i + 1) % count) for i in range(ends)])]
    reduce_sum x5 -> x0, other arithmetic: 12.5 us -> none  [the longest x3 12.2 us: depth_grad(): jnp.sum(grads_f * window.astype(jnp.float32), axis=(1, 2, 3))]
    convert_element_type x2 -> x0, other arithmetic: 11.7 us -> none  [the longest x1 5.85 us: local(): depth_apply(pad_planes(grad_border), per_channel_kernel, array_shape, True)]
    slice x18 -> x0, local copies, waits for them, and re-layouts: 10.3 us -> none  [the longest x8 6.53 us: extended(): lax.slice_in_dim(cells, cells.shape[dim] - width, cells.shape[dim], axis=...]
    another operation x28 -> x0, local copies, waits for them, and re-layouts: 9.56 us -> none  [depth_grad(): return jnp.stack(columns, axis=1)]
  transfers between devices with their start and end apart: 9 -> 0, of which waited for: 5 -> 0; matrix products, arithmetic and copies ran while one was open for 3% -> 0% of each run, Pallas kernels for 0% -> 0%
where the time goes in v2:
time: 69.6 us; the launch traced here: 69.5 us
  Pallas kernels  63.1 us (91%)
  local copies, waits for them, and re-layouts  5.75 us (8%)
    pallas_call x1, Pallas kernels, local(): pl.pallas_call(functools.partial(kernel, (n_col, n_bulk), scale), out_sha...  63.1 us
    unnamed x10, local copies, waits for them, and re-layouts  3.93 us
    transpose x1, local copies, waits for them, and re-layouts, local(): jnp.transpose(g, (2, 1, 0, 3))  1.81 us

profile of v2, /device:TPU:1, one launch (start us, length us, event | category | flops | bytes accessed | tf_op | source)
XLA Modules:
  0.0 69.5 jit_solution(13225952190583221284)
XLA Ops:
  0.6 1.8 %copy_bitcast_fusion = (bf16[2,4,96,128]{3,2,1,0:T(8,128)(2,1)}, bf16[2,4,96,128]{3,2,1,0:T(8,128)(2,1)}) fusion(bf16[96,4,2,128]{3,2,1,0:T(2,128)(2,1)} %param.8, bf16[96,4,2,128]{3,2,1,0:T(2,128)(2,1)} %param.7), kind=kLoop, calls=%fused_computation | loop fusion | bytes 786432 | tf_op jit(solution)/shard_map/transpose | solution.py:589
  2.4 63.1 %shard_map.102 = (bf16[2,4,96,128]{3,2,1,0:T(8,128)(2,1)}, f32[288,96]{1,0:T(8,128)}, f32[288,27]{1,0:T(8,128)}, f32[2]{0:T(128)}) custom-call(bf16[2,4,96,128]{3,2,1,0:T(8,128)(2,1)} %get-tuple-element.17.x_ref, bf16[2,4,96,128]{3,2,1,0:T(8,128)(2,1)} %get-tuple-element.16.g_ref, bf16[288,96]{1,0:T(8,128)(2,1)} %w_ref.1, f32[27,288]{1,0:T(8,128)} %bitcast.7, ...), custom_call_target="tpu_custom_call" | custom-call | tf_op jit(solution)/shard_map/pallas_call | solution.py:545
  65.5 0.0 copy-start.1
  65.5 1.8 %copy.13 = bf16[96,4,2,128]{3,2,1,0:T(2,128)(2,1)} copy(bf16[96,4,2,128]{3,0,1,2:T(8,128)(2,1)} %bitcast.6) | data formatting | bytes 393216
  67.4 0.0 copy-done.1
  67.4 0.0 copy-start
  67.4 0.7 %copy.14 = f32[288,27]{0,1:T(8,128)} copy(f32[288,27]{1,0:T(8,128)S(1)} %copy-done.1) | data formatting | bytes 62208
  68.1 0.2 copy-done
  68.3 0.0 copy-start.2
  68.3 0.7 copy.19
  69.0 0.0 copy-done.2
  69.0 0.5 copy.20
Async XLA Ops:
  65.5 1.9 %copy-start.1 = (f32[288,27]{1,0:T(8,128)S(1)}, f32[288,27]{1,0:T(8,128)}, u32[]{:S(2)}) copy-start(f32[288,27]{1,0:T(8,128)} %get-tuple-element.14) | copy-start | bytes 93316
  67.4 0.9 %copy-start = (f32[288,96]{1,0:T(8,128)S(1)}, f32[288,96]{1,0:T(8,128)}, u32[]{:S(2)}) copy-start(f32[288,96]{1,0:T(8,128)} %get-tuple-element.23) | copy-start | bytes 331780
  68.3 0.7 copy-start.2

commit v3 on v2

--- a/solution.py
+++ b/solution.py
@@ -17,6 +17,7 @@
 C3 = 3 * C
 LANES = 128
 CHUNK = 32
+DEPTH_CHUNK = 32
 EDGE_COLUMNS = (0, 1, LANES - 2, LANES - 1)
 NEIGHBOURS = [(a, b) for a in (-1, 0, 1) for b in (-1, 0, 1)]
 
@@ -82,69 +83,76 @@
     )
 
 
-def each(count, what):
-    def body(step, carry):
-        what(step)
-        return carry
-
-    lax.fori_loop(1, count, body, 0)
+def ring_distance(step, count):
+    return min(step, count - step)
+
+
+def bulk_peers(bulk, n_bulk):
+    if n_bulk != 32:
+        return [lax.rem(bulk + step, n_bulk) for step in range(1, n_bulk)]
+    ys = [lax.rem(bulk // 8 + d, 4) * 8 for d in range(4)]
+    xs = [lax.rem(lax.rem(bulk // 2, 4) + d, 4) * 2 for d in range(4)]
+    cores = [lax.rem(bulk + d, 2) for d in range(2)]
+    steps = [(y, x, c) for y in range(4) for x in range(4) for c in range(2)][1:]
+    steps.sort(key=lambda t: -2 * ring_distance(t[0], 4) - 2 * ring_distance(t[1], 4) - t[2])
+    return [ys[y] + xs[x] + cores[c] for y, x, c in steps]
+
+
+def col_peers(col, n_col):
+    steps = sorted(range(1, n_col), key=lambda d: -ring_distance(d, n_col))
+    return [lax.rem(col + d, n_col) for d in steps]
 
 
 class Reduction:
-    def __init__(self, sizes, place, pack, parts, planes, whole, sems):
-        self.n_col, self.n_bulk = sizes
+    def __init__(self, place, peers, pack, parts, planes, whole, sems):
         self.col, self.bulk = place
+        self.in_plane, self.in_col = peers
         self.pack, self.parts, self.planes, self.whole = pack, parts, planes, whole
         self.s_send, self.s_recv, self.z_send, self.z_recv, self.g_send, self.g_recv = sems
 
-    def bulk_peer(self, step):
-        return lax.rem(self.bulk + step, self.n_bulk)
-
-    def col_peer(self, step):
-        return lax.rem(self.col + step, self.n_col)
-
-    def scatter(self, step, incoming=False):
-        peer = self.bulk_peer(step)
-        slot = peer if incoming else self.bulk
-        return remote(
-            self.pack.at[peer], self.parts.at[slot], self.s_send.at[peer], self.s_recv.at[slot], (self.col, peer)
-        )
-
-    def across(self, step, incoming=False):
-        peer = self.col_peer(step)
-        slot = peer if incoming else self.col
-        return remote(
-            self.planes.at[slot], self.planes.at[slot], self.z_send.at[peer], self.z_recv.at[slot], (peer, self.bulk)
-        )
-
-    def spread(self, step, incoming=False):
-        peer = self.bulk_peer(step)
-        slot = peer if incoming else self.bulk
-        return remote(
-            self.whole.at[slot], self.whole.at[slot], self.g_send.at[peer], self.g_recv.at[slot], (self.col, peer)
-        )
+    def scattered(self):
+        rest = pl.ds(0, len(self.in_plane))
+        target = (self.col, self.in_plane[0])
+        return remote(self.pack.at[rest], self.parts.at[rest], self.s_send, self.s_recv, target)
+
+    def crossed(self):
+        rest = pl.ds(0, len(self.in_col))
+        target = (self.in_col[0], self.bulk)
+        return remote(self.planes.at[rest], self.planes.at[rest], self.z_send, self.z_recv, target)
+
+    def gathered(self):
+        rest = pl.ds(0, len(self.in_plane))
+        target = (self.col, self.in_plane[0])
+        return remote(self.whole.at[rest], self.whole.at[rest], self.g_send, self.g_recv, target)
 
     def start(self):
-        each(self.n_bulk, lambda step: self.scatter(step).start())
+        for peer in self.in_plane:
+            remote(
+                self.pack.at[peer], self.parts.at[self.bulk], self.s_send, self.s_recv, (self.col, peer)
+            ).start()
         self.parts[self.bulk] = self.pack[self.bulk]
 
     def middle(self):
-        each(self.n_bulk, lambda step: self.scatter(step, True).wait_recv())
+        self.scattered().wait_recv()
         self.planes[self.col] = jnp.sum(self.parts[...], axis=0)
-        each(self.n_col, lambda step: self.across(step).start())
+        mine = self.planes.at[self.col]
+        for peer in self.in_col:
+            remote(mine, mine, self.z_send, self.z_recv, (peer, self.bulk)).start()
 
     def final(self):
-        each(self.n_col, lambda step: self.across(step, True).wait_recv())
+        self.crossed().wait_recv()
         self.whole[self.bulk] = jnp.sum(self.planes[...], axis=0)
-        each(self.n_bulk, lambda step: self.spread(step).start())
+        mine = self.whole.at[self.bulk]
+        for peer in self.in_plane:
+            remote(mine, mine, self.g_send, self.g_recv, (self.col, peer)).start()
 
     def finish(self):
-        each(self.n_bulk, lambda step: self.spread(step, True).wait_recv())
+        self.gathered().wait_recv()
 
     def drain(self):
-        each(self.n_bulk, lambda step: self.scatter(step).wait_send())
-        each(self.n_col, lambda step: self.across(step).wait_send())
-        each(self.n_bulk, lambda step: self.spread(step).wait_send())
+        self.scattered().wait_send()
+        self.crossed().wait_send()
+        self.gathered().wait_send()
 
 
 def conv(source, y0, weights, flip, sink):
@@ -171,8 +179,8 @@
 def kernel(
     sizes,
     scale,
-    x_ref,
-    g_ref,
+    x_in,
+    g_in,
     w_ref,
     k_ref,
     sharp_ref,
@@ -182,6 +190,8 @@
     pd_ref,
     kd_ref,
     sd_ref,
+    x_ref,
+    g_ref,
     xh,
     gh,
     messages,
@@ -220,8 +230,9 @@
 ):
     n_col, n_bulk = sizes
     col, bulk = lax.axis_index("col"), lax.axis_index("bulk")
-    first = Reduction(sizes, (col, bulk), pack1, parts1, planes1, whole1, sems[:6])
-    second = Reduction(sizes, (col, bulk), pack2, parts2, planes2, whole2, sems[6:])
+    peers = bulk_peers(bulk, n_bulk), col_peers(col, n_col)
+    first = Reduction((col, bulk), peers, pack1, parts1, planes1, whole1, sems[:6])
+    second = Reduction((col, bulk), peers, pack2, parts2, planes2, whole2, sems[6:])
     low, high = bulk > 0, bulk < n_bulk - 1
 
     xh[...] = jnp.zeros_like(xh)
@@ -232,12 +243,19 @@
     def greet(target):
         pl.semaphore_signal(barrier, inc=1, device_id=target, device_id_type=MESH)
 
-    each(n_bulk, lambda step: greet((col, lax.rem(bulk + step, n_bulk))))
-    each(n_col, lambda step: greet((lax.rem(col + step, n_col), bulk)))
     for a in (1, n_col - 1):
         for b in (1, n_bulk - 1):
             greet((lax.rem(col + a, n_col), lax.rem(bulk + b, n_bulk)))
-
+    for peer in reversed(peers[1]):
+        greet((peer, bulk))
+    for peer in reversed(peers[0]):
+        greet((col, peer))
+
+    for source, planes in ((x_in, x_ref), (g_in, g_ref)):
+        for z in range(4):
+            pair = source[:, z].astype(F32)
+            for y in range(2):
+                planes[y, z] = pair[:, y, :].astype(BF16)
     row32, lane32 = iota((32, LANES), 0), iota((32, LANES), 1)
     for k, source in enumerate((x_ref, g_ref)):
         total = jnp.zeros((32, C), F32)
@@ -250,13 +268,6 @@
         messages[k] = jnp.zeros((32, LANES), BF16)
         messages[k, :, 0:C] = total.astype(BF16)
 
-    taps_t[...] = jnp.zeros_like(taps_t)
-    taps_t[0:27, 0:C3] = k_ref[...]
-    for j in range(3):
-        taps_c[LANES * j : LANES * (j + 1), :] = taps_t[:, LANES * j : LANES * (j + 1)].T
-    for t in range(27):
-        weights[t] = jnp.broadcast_to(taps_c[0:C3, t : t + 1], (C3, LANES))
-
     pl.semaphore_wait(barrier, n_bulk + n_col - 2 + 4)
 
     def row_copy(k, down):
@@ -288,23 +299,8 @@
         pl.when(low)(lambda: row_copy(k, True).wait_recv())
         pl.when(high)(lambda: row_copy(k, False).wait_recv())
 
-    for (a, b) in NEIGHBOURS:
-        if (a, b) != (0, 0):
-            pl.when(inside(a, b))(lambda a=a, b=b: edge_copy(-a, -b).wait_recv())
-
-    for c in range(3):
-        edge_t[c] = dot(
-            place_ref[LANES * c : LANES * (c + 1), :], arrived[:, 0].reshape(9 * 32, LANES)
-        ).astype(BF16)
-    edge_t[3] = dot(place_ref[LANES : 2 * LANES, :], arrived[:, 1].reshape(9 * 32, LANES)).astype(BF16)
-    eye = jnp.where(iota((LANES, LANES), 0) == iota((LANES, LANES), 1), 1.0, 0.0).astype(BF16)
-    edge_x[...] = dot_nt(eye, edge_t[1])
-    edge_g[...] = dot_nt(eye, edge_t[3]).astype(BF16)
-    for c in range(3):
-        field_edge[c] = rounded(dot_nt(w_ref[...], edge_t[c, :, 0:C]))
-
     def turned(values, z, y):
-        return pltpu.roll(values, LANES - 13 - 2 * (y + 2) - 12 * z, 1)
+        return pltpu.roll(values, LANES - 1 - 2 * edge_index(z, y), 1)
 
     def shifted(values, edge):
         lane = iota(values.shape, 1)
@@ -316,17 +312,16 @@
         return x_ref.at[y] if y in (0, 1) else xh.at[{-2: 0, -1: 1, 2: 2, 3: 3}[y]]
 
     def make_field(ys):
-        def body(z, carry):
-            for y in ys:
+        for y in ys:
+            for z in range(4):
                 plane = input_row(y)[z]
-                before, after = shifted(plane.astype(F32), turned(edge_x[0:C, :], z, y))
+                wide = plane.astype(F32)
+                edge = wide if y in (0, 1) else turned(edge_x[0:C, :], z, y)
+                before, after = shifted(wide, edge)
                 cells = jnp.concatenate([before.astype(BF16), plane, after.astype(BF16)], axis=1)
                 made = rounded(dot(w_ref[...], cells))
                 for c in range(3):
                     field[c, y + 2, z] = made[:, LANES * c : LANES * (c + 1)]
-            return carry
-
-        lax.fori_loop(0, 4, body, 0)
 
     def make_mixed(y):
         def sink(z, rows, value):
@@ -334,7 +329,30 @@
 
         conv(field, y + 1, weights, False, sink)
 
+    taps_t[...] = jnp.zeros_like(taps_t)
+    taps_t[0:27, 0:C3] = k_ref[...]
+    for j in range(3):
+        taps_c[LANES * j : LANES * (j + 1), :] = taps_t[:, LANES * j : LANES * (j + 1)].T
+    for t in range(27):
+        weights[t] = jnp.broadcast_to(taps_c[0:C3, t : t + 1], (C3, LANES))
+
     make_field((0, 1))
+    for (a, b) in NEIGHBOURS:
+        if (a, b) != (0, 0):
+            pl.when(inside(a, b))(lambda a=a, b=b: edge_copy(-a, -b).wait_recv())
+
+    def placed(c, kind):
+        return dot(place_ref[LANES * c : LANES * (c + 1), :], arrived[:, kind].reshape(9 * 32, LANES)).astype(BF16)
+
+    eye = jnp.where(iota((LANES, LANES), 0) == iota((LANES, LANES), 1), 1.0, 0.0).astype(BF16)
+    edge_t[1] = placed(1, 0)
+    edge_x[...] = dot_nt(eye, edge_t[1])
+    field_edge[1] = rounded(dot_nt(w_ref[...], edge_t[1, :, 0:C]))
+    for y in range(2):
+        for z in range(4):
+            edge = turned(field_edge[1], z, y)
+            field[0, y + 2, z, :, 0:1] = edge[:, 0:1]
+            field[2, y + 2, z, :, LANES - 1 : LANES] = edge[:, LANES - 1 : LANES]
     wait_row(0)
     make_field((-1, 2))
     make_mixed(0)
@@ -369,6 +387,11 @@
 
     wait_row(1)
     make_field((-2, 3))
+    for c in (0, 2):
+        edge_t[c] = placed(c, 0)
+        field_edge[c] = rounded(dot_nt(w_ref[...], edge_t[c, :, 0:C]))
+    edge_t[3] = placed(1, 1)
+    edge_g[...] = dot_nt(eye, edge_t[3]).astype(BF16)
     spread_edge = []
     for a in range(3):
         for b in range(3):
@@ -446,7 +469,7 @@
     for part in range(3):
         grads_edge[C * part : C * (part + 1), :] = jnp.where(mask > 0.5, rounded(edges[part]), 0.0)
 
-    def grad_planes(z, carry):
+    def grad_planes(z):
         for y in range(-1, 3):
             g = g_ref[y, z] if y in (0, 1) else gh[0 if y == -1 else 1, z]
             made = gradients(mixed[y + 1, z, 0:C, :], mixed[y + 1, z, C : 2 * C, :], g)
@@ -461,9 +484,9 @@
                 grads[0, y + 1, z, rows, :] = before
                 grads[1, y + 1, z, rows, :] = plane
                 grads[2, y + 1, z, rows, :] = after
-        return carry
-
-    lax.fori_loop(0, 4, grad_planes, 0)
+
+    for z in range(4):
+        grad_planes(z)
 
     for y in range(2):
 
@@ -479,32 +502,34 @@
     pay2[:, 0:C] = weight
 
     def depth(j, carry):
-        rows = pl.ds(pl.multiple_of(j * CHUNK, CHUNK), CHUNK)
-        lane = iota((CHUNK, LANES), 1)
+        rows = pl.ds(pl.multiple_of(j * DEPTH_CHUNK, DEPTH_CHUNK), DEPTH_CHUNK)
+        lane = iota((DEPTH_CHUNK, LANES), 1)
         made = pay2[rows, :]
+        mine = [[grads[1, y + 1, z, rows, :] for z in range(4)] for y in range(2)]
         for b in range(3):
             for c in range(3):
+                cells = [[field[c, y + b + 1, z, rows, :] for z in range(4)] for y in range(2)]
                 for a in range(3):
                     total = None
                     for y in range(2):
                         for z in range(4):
                             if 0 <= z + a - 1 < 4:
-                                term = grads[1, y + 1, z, rows, :] * field[c, y + b + 1, z + a - 1, rows, :]
+                                term = mine[y][z] * cells[y][z + a - 1]
                                 total = term if total is None else total + term
                     tap = 9 * a + 3 * b + c
                     made = jnp.where(lane == C + tap, jnp.sum(total, axis=1, keepdims=True), made)
         pay2[rows, :] = jnp.where(lane < C + 27, made, 0.0)
         return carry
 
-    lax.fori_loop(0, C3 // CHUNK, depth, 0)
+    lax.fori_loop(0, C3 // DEPTH_CHUNK, depth, 0)
     rows2 = C3 // n_bulk
     for i in range(n_bulk):
         pack2[i] = pay2[rows2 * i : rows2 * (i + 1), :]
     second.start()
 
-    for y in range(2):
-        for z in range(4):
-            dx_ref[y, z] = dot_tn(w_ref[...], field_grad[y, z]).astype(BF16)
+    for z in range(4):
+        rows_y = [dot_tn(w_ref[...], field_grad[y, z]) for y in range(2)]
+        dx_ref[:, z] = jnp.stack(rows_y, axis=1).astype(BF16)
     for k in range(3):
         pl.when(high)(lambda k=k: row_copy(k, True).wait_send())
         pl.when(low)(lambda k=k: row_copy(k, False).wait_send())
@@ -518,8 +543,19 @@
     for i in range(n_bulk):
         pay2[rows2 * i : rows2 * (i + 1), :] = whole2[i]
     pd_ref[...] = pay2[:, 0:C] * scale
-    kd_ref[...] = pay2[:, C : C + 27] * scale
+    taps_c[0:C3, :] = pay2[...] * scale
+    for j in range(3):
+        taps_t[:, LANES * j : LANES * (j + 1)] = taps_c[LANES * j : LANES * (j + 1), :].T
+    kd_ref[...] = taps_t[C : C + 27, 0:C3]
     second.drain()
+
+
+def hand_out(dx_in, pd_in, kd_in, sd_in, dx_ref, pd_ref, kd_ref, sd_ref):
+    dx_ref[...] = dx_in[...]
+    pd_ref[...] = pd_in[...]
+    kd_ref[...] = kd_in[...]
+    for e in range(2):
+        sd_ref[e] = sd_in[e]
 
 
 def local(x, g, w, k, sharp):
@@ -541,18 +577,20 @@
     def dma(count):
         return pltpu.SemaphoreType.DMA((count,))
 
-    reduction_sems = [dma(n_bulk), dma(n_bulk), dma(n_col), dma(n_col), dma(n_bulk), dma(n_bulk)]
+    reduction_sems = [pltpu.SemaphoreType.DMA] * 6
     dx, pd, kd, sd = pl.pallas_call(
         functools.partial(kernel, (n_col, n_bulk), scale),
         out_shape=(
-            jax.ShapeDtypeStruct((2, 4, C, LANES), BF16),
+            jax.ShapeDtypeStruct((C, 4, 2, LANES), BF16),
             jax.ShapeDtypeStruct((C3, C), F32),
-            jax.ShapeDtypeStruct((C3, 27), F32),
+            jax.ShapeDtypeStruct((27, C3), F32),
             jax.ShapeDtypeStruct((2,), F32),
         ),
         in_specs=[vmem, vmem, vmem, vmem, smem, vmem, vmem],
         out_specs=(vmem, vmem, vmem, smem),
         scratch_shapes=[
+            pltpu.VMEM((2, 4, C, LANES), BF16),
+            pltpu.VMEM((2, 4, C, LANES), BF16),
             pltpu.VMEM((4, 4, C, LANES), BF16),
             pltpu.VMEM((2, 4, C, LANES), BF16),
             pltpu.VMEM((2, 32, LANES), BF16),
@@ -585,15 +623,21 @@
             collective_id=0, has_side_effects=True, vmem_limit_bytes=56 * 2**20
         ),
     )(
-        jnp.transpose(x, (2, 1, 0, 3)),
-        jnp.transpose(g, (2, 1, 0, 3)),
+        x,
+        g,
         w,
         k.T,
         sharp,
         jnp.asarray(place, BF16),
         jnp.asarray(flags),
     )
-    return jnp.transpose(dx, (2, 1, 0, 3)), pd, kd, sd
+    dx, pd, kd, sd = pl.pallas_call(
+        hand_out,
+        out_shape=tuple(jax.ShapeDtypeStruct(v.shape, v.dtype) for v in (dx, pd, kd, sd)),
+        in_specs=[vmem, vmem, vmem, smem],
+        out_specs=(vmem, vmem, vmem, smem),
+    )(dx, pd, kd, sd)
+    return dx, pd, kd.T, sd
 
 
 def solution(mesh):

time: 69.6 us -> 58.8 us (0.84)
  local copies, waits for them, and re-layouts: 5.75 us -> 0 us
  Pallas kernels: 63.1 us -> 58 us
    pallas_call x1, Pallas kernels: 63.1 us -> 56.2 us  [local(): pl.pallas_call(functools.partial(kernel, (n_col, n_bulk), scale), out_sha...]
    unnamed x10 -> x0, local copies, waits for them, and re-layouts: 3.93 us -> none
    transpose x1 -> x0, local copies, waits for them, and re-layouts: 1.81 us -> none  [local(): jnp.transpose(g, (2, 1, 0, 3))]
    pallas_call x0 -> x1, Pallas kernels: none -> 1.76 us  [local(): pl.pallas_call(hand_out, out_shape=tuple((jax.ShapeDtypeStruct(v.shape, v...]
where the time goes in v3:
time: 58.8 us; the launch traced here: 58.6 us
  Pallas kernels  58 us (99%)
  between operations  0.64 us (1%)
    pallas_call x1, Pallas kernels, local(): pl.pallas_call(functools.partial(kernel, (n_col, n_bulk), scale), out_sha...  56.2 us
    pallas_call x1, Pallas kernels, local(): pl.pallas_call(hand_out, out_shape=tuple((jax.ShapeDtypeStruct(v.shape, v...  1.76 us

profile of v3, /device:TPU:1, one launch (start us, length us, event | category | flops | bytes accessed | tf_op | source)
XLA Modules:
  0.0 58.6 jit_solution(6260936868901853422)
XLA Ops:
  0.6 56.2 %shard_map.102 = (bf16[96,4,2,128]{3,2,1,0:T(2,128)(2,1)}, f32[288,96]{1,0:T(8,128)}, f32[27,288]{1,0:T(8,128)}, f32[2]{0:T(128)}) custom-call(bf16[96,4,2,128]{3,2,1,0:T(2,128)(2,1)} %x_in.1, bf16[96,4,2,128]{3,2,1,0:T(2,128)(2,1)} %g_in.1, bf16[288,96]{1,0:T(8,128)(2,1)} %w_ref.1, f32[27,288]{1,0:T(8,128)} %bitcast.2, f32[2]{0:T(128)} %sharp_ref.1, ...), custom_call_target="tpu_custom_call" | custom-call | tf_op jit(solution)/shard_map/pallas_call | solution.py:581
  56.9 1.8 %shard_map.103 = (bf16[96,4,2,128]{3,2,1,0:T(2,128)(2,1)}, f32[288,96]{1,0:T(8,128)}, f32[27,288]{1,0:T(8,128)}, f32[2]{0:T(128)}) custom-call(bf16[96,4,2,128]{3,2,1,0:T(2,128)(2,1)} %get-tuple-element.12.dx_in, f32[288,96]{1,0:T(8,128)} %get-tuple-element.13.pd_in, f32[27,288]{1,0:T(8,128)} %get-tuple-element.14.kd_in, f32[2]{0:T(128)} %get-tuple-element.15.sd_in), custom_call_target="tpu_custom_call" | custom-call | tf_op jit(solution)/shard_map/pallas_call | solution.py:634

commit v4 on v3

--- a/solution.py
+++ b/solution.py
@@ -17,7 +17,7 @@
 C3 = 3 * C
 LANES = 128
 CHUNK = 32
-DEPTH_CHUNK = 32
+EARLY_TAPS = 10
 EDGE_COLUMNS = (0, 1, LANES - 2, LANES - 1)
 NEIGHBOURS = [(a, b) for a in (-1, 0, 1) for b in (-1, 0, 1)]
 
@@ -155,11 +155,11 @@
         self.gathered().wait_send()
 
 
-def conv(source, y0, weights, flip, sink):
+def conv(source, y0, weights, flip, sink, bs=(0, 1, 2), start=None):
     def body(j, carry):
         rows = pl.ds(pl.multiple_of(j * CHUNK, CHUNK), CHUNK)
-        total = [None] * 4
-        for b in range(3):
+        total = [None if start is None else start(z, rows) for z in range(4)]
+        for b in bs:
             for c in range(3):
                 cells = [source[c, y0 + b, z, rows, :] for z in range(4)]
                 for a in range(3):
@@ -179,17 +179,23 @@
 def kernel(
     sizes,
     scale,
-    x_in,
-    g_in,
-    w_ref,
-    k_ref,
+    x_hbm,
+    g_hbm,
+    w_hbm,
+    k_hbm,
     sharp_ref,
-    place_ref,
+    place_hbm,
     flags_ref,
     dx_ref,
     pd_ref,
     kd_ref,
     sd_ref,
+    x_in,
+    g_in,
+    w_ref,
+    k_ref,
+    place_ref,
+    load_sem,
     x_ref,
     g_ref,
     xh,
@@ -210,6 +216,7 @@
     grads_edge,
     field_grad,
     turn,
+    partial,
     couple,
     coef,
     pay1,
@@ -235,6 +242,15 @@
     second = Reduction((col, bulk), peers, pack2, parts2, planes2, whole2, sems[6:])
     low, high = bulk > 0, bulk < n_bulk - 1
 
+    loads = [
+        pltpu.make_async_copy(source, target, load_sem.at[i])
+        for i, (source, target) in enumerate(
+            ((x_hbm, x_in), (g_hbm, g_in), (w_hbm, w_ref), (k_hbm, k_ref), (place_hbm, place_ref))
+        )
+    ]
+    for load in loads:
+        load.start()
+
     xh[...] = jnp.zeros_like(xh)
     gh[...] = jnp.zeros_like(gh)
     arrived[...] = jnp.zeros_like(arrived)
@@ -251,23 +267,42 @@
     for peer in reversed(peers[0]):
         greet((col, peer))
 
-    for source, planes in ((x_in, x_ref), (g_in, g_ref)):
+    row32, lane32 = iota((32, LANES), 0), iota((32, LANES), 1)
+
+    def take_in(kind):
+        source, planes = (x_in, g_in)[kind], (x_ref, g_ref)[kind]
+        loads[kind].wait()
         for z in range(4):
             pair = source[:, z].astype(F32)
             for y in range(2):
                 planes[y, z] = pair[:, y, :].astype(BF16)
-    row32, lane32 = iota((32, LANES), 0), iota((32, LANES), 1)
-    for k, source in enumerate((x_ref, g_ref)):
+
+    def make_messages(kind):
+        planes = (x_ref, g_ref)[kind]
         total = jnp.zeros((32, C), F32)
         for y in range(2):
             for z in range(4):
                 pick = jnp.zeros((32, LANES), jnp.bool_)
                 for s, column in enumerate(EDGE_COLUMNS):
                     pick = pick | ((row32 == s * 8 + y * 4 + z) & (lane32 == column))
-                total = total + dot_nt(jnp.where(pick, 1.0, 0.0).astype(BF16), source[y, z])
-        messages[k] = jnp.zeros((32, LANES), BF16)
-        messages[k, :, 0:C] = total.astype(BF16)
-
+                total = total + dot_nt(jnp.where(pick, 1.0, 0.0).astype(BF16), planes[y, z])
+        messages[kind] = jnp.zeros((32, LANES), BF16)
+        messages[kind, :, 0:C] = total.astype(BF16)
+
+    take_in(0)
+    make_messages(0)
+
+    loads[3].wait()
+    taps_t[...] = jnp.zeros_like(taps_t)
+    taps_t[0:27, 0:C3] = k_ref[...]
+    for j in range(3):
+        taps_c[LANES * j : LANES * (j + 1), :] = taps_t[:, LANES * j : LANES * (j + 1)].T
+
+    def spread_taps(which):
+        for t in which:
+            weights[t] = jnp.broadcast_to(taps_c[0:C3, t : t + 1], (C3, LANES))
+
+    spread_taps(range(EARLY_TAPS))
     pl.semaphore_wait(barrier, n_bulk + n_col - 2 + 4)
 
     def row_copy(k, down):
@@ -279,21 +314,33 @@
         sem = 2 * k + (1 if down else 0)
         return remote(source, target, row_send.at[sem], row_recv.at[sem], (col, lax.rem(bulk + (1 if down else n_bulk - 1), n_bulk)))
 
-    def edge_copy(a, b):
+    def edge_copy(kind, a, b):
         slot = slot_of(-a, -b)
         target = (lax.rem(col + a + n_col, n_col), lax.rem(bulk + b + n_bulk, n_bulk))
-        return remote(messages, arrived.at[slot], edge_send.at[slot], edge_recv.at[slot], target)
+        sem = 9 * kind + slot
+        return remote(messages.at[kind], arrived.at[kind, slot], edge_send.at[sem], edge_recv.at[sem], target)
 
     def inside(a, b):
         return (col + a >= 0) & (col + a < n_col) & (bulk + b >= 0) & (bulk + b < n_bulk)
 
-    for (a, b) in NEIGHBOURS:
-        if (a, b) != (0, 0):
-            pl.when(inside(a, b))(lambda a=a, b=b: edge_copy(a, b).start())
-    for k in range(3):
-        pl.when(high)(lambda k=k: row_copy(k, True).start())
-        pl.when(low)(lambda k=k: row_copy(k, False).start())
-    arrived[slot_of(0, 0)] = messages[...]
+    around = [(a, b) for (a, b) in NEIGHBOURS if (a, b) != (0, 0)]
+    around.sort(key=lambda t: -abs(t[0]) - abs(t[1]))
+
+    def send_edges(kind):
+        for (a, b) in around:
+            pl.when(inside(a, b))(lambda a=a, b=b: edge_copy(kind, a, b).start())
+        arrived[kind, slot_of(0, 0)] = messages[kind]
+
+    def wait_edges(kind):
+        for (a, b) in around:
+            pl.when(inside(a, b))(lambda a=a, b=b: edge_copy(kind, -a, -b).wait_recv())
+
+    def send_row(k):
+        pl.when(high)(lambda: row_copy(k, True).start())
+        pl.when(low)(lambda: row_copy(k, False).start())
+
+    send_edges(0)
+    send_row(0)
 
     def wait_row(k):
         pl.when(low)(lambda: row_copy(k, True).wait_recv())
@@ -311,52 +358,73 @@
     def input_row(y):
         return x_ref.at[y] if y in (0, 1) else xh.at[{-2: 0, -1: 1, 2: 2, 3: 3}[y]]
 
-    def make_field(ys):
+    def make_field(ys, edged):
         for y in ys:
             for z in range(4):
                 plane = input_row(y)[z]
                 wide = plane.astype(F32)
-                edge = wide if y in (0, 1) else turned(edge_x[0:C, :], z, y)
+                edge = turned(edge_x[0:C, :], z, y) if edged else 0.0
                 before, after = shifted(wide, edge)
                 cells = jnp.concatenate([before.astype(BF16), plane, after.astype(BF16)], axis=1)
                 made = rounded(dot(w_ref[...], cells))
                 for c in range(3):
                     field[c, y + 2, z] = made[:, LANES * c : LANES * (c + 1)]
 
+    def gather(y, bs, start):
+        def sink(z, rows, value):
+            partial[y, z, rows, :] = value
+
+        conv(field, y + 1, weights, False, sink, bs, start)
+
     def make_mixed(y):
         def sink(z, rows, value):
             mixed[y + 1, z, rows, :] = value.astype(BF16)
 
         conv(field, y + 1, weights, False, sink)
 
-    taps_t[...] = jnp.zeros_like(taps_t)
-    taps_t[0:27, 0:C3] = k_ref[...]
-    for j in range(3):
-        taps_c[LANES * j : LANES * (j + 1), :] = taps_t[:, LANES * j : LANES * (j + 1)].T
-    for t in range(27):
-        weights[t] = jnp.broadcast_to(taps_c[0:C3, t : t + 1], (C3, LANES))
-
-    make_field((0, 1))
-    for (a, b) in NEIGHBOURS:
-        if (a, b) != (0, 0):
-            pl.when(inside(a, b))(lambda a=a, b=b: edge_copy(-a, -b).wait_recv())
+    for load in (loads[2], loads[4]):
+        load.wait()
+    spread_taps(range(EARLY_TAPS, 27))
+
+    make_field((0, 1), False)
+    gather(0, (1, 2), None)
+    gather(1, (0, 1), None)
+    take_in(1)
+    wait_row(0)
+    for k in (1, 2):
+        send_row(k)
+    make_field((-1, 2), False)
+    gather(0, (0,), lambda z, rows: partial[0, z, rows, :])
+    gather(1, (2,), lambda z, rows: partial[1, z, rows, :])
+    wait_edges(0)
 
     def placed(c, kind):
-        return dot(place_ref[LANES * c : LANES * (c + 1), :], arrived[:, kind].reshape(9 * 32, LANES)).astype(BF16)
+        return dot(place_ref[LANES * c : LANES * (c + 1), :], arrived[kind].reshape(9 * 32, LANES)).astype(BF16)
 
     eye = jnp.where(iota((LANES, LANES), 0) == iota((LANES, LANES), 1), 1.0, 0.0).astype(BF16)
     edge_t[1] = placed(1, 0)
-    edge_x[...] = dot_nt(eye, edge_t[1])
     field_edge[1] = rounded(dot_nt(w_ref[...], edge_t[1, :, 0:C]))
-    for y in range(2):
-        for z in range(4):
-            edge = turned(field_edge[1], z, y)
-            field[0, y + 2, z, :, 0:1] = edge[:, 0:1]
-            field[2, y + 2, z, :, LANES - 1 : LANES] = edge[:, LANES - 1 : LANES]
-    wait_row(0)
-    make_field((-1, 2))
-    make_mixed(0)
-    make_mixed(1)
+
+    lane = iota((C, LANES), 1)
+    left = lax.rem(lane, 2) == 1
+    outer = (lane == 0) | (lane == LANES - 1)
+    for j in range(3):
+        rows = slice(C * j, C * (j + 1))
+        beside = field_edge[1, rows, :]
+        along_y = [pltpu.roll(beside, 2, 1), beside, pltpu.roll(beside, LANES - 2, 1)]
+        along_z = []
+        for a in range(3):
+            part = None
+            for b in range(3):
+                tap = 9 * a + 3 * b
+                term = jnp.where(left, weights[tap, rows, :], weights[tap + 2, rows, :]) * along_y[b]
+                part = term if part is None else part + term
+            along_z.append(part)
+        part = along_z[1] + (pltpu.roll(along_z[0], 12, 1) + pltpu.roll(along_z[2], LANES - 12, 1))
+        for y in range(2):
+            for z in range(4):
+                value = partial[y, z, rows, :] + jnp.where(outer, turned(part, z, y), 0.0)
+                mixed[y + 1, z, rows, :] = value.astype(BF16)
 
     row, lane = iota((C, LANES), 0), iota((C, LANES), 1)
     upper = row < HEAD
@@ -385,28 +453,43 @@
         pack1[i] = pay1[rows1 * i : rows1 * (i + 1), :]
     first.start()
 
+    make_messages(1)
+    send_edges(1)
     wait_row(1)
-    make_field((-2, 3))
+    edge_x[...] = dot_nt(eye, edge_t[1])
+    make_field((-2, 3), True)
+    for y in range(-1, 3):
+        for z in range(4):
+            edge = turned(field_edge[1], z, y)
+            field[0, y + 2, z, :, 0:1] = edge[:, 0:1]
+            field[2, y + 2, z, :, LANES - 1 : LANES] = edge[:, LANES - 1 : LANES]
     for c in (0, 2):
         edge_t[c] = placed(c, 0)
         field_edge[c] = rounded(dot_nt(w_ref[...], edge_t[c, :, 0:C]))
+    for j in range(3):
+        rows = slice(C * j, C * (j + 1))
+        along_z = []
+        for a in range(3):
+            along_y = []
+            for b in range(3):
+                part = None
+                for c in range(3):
+                    term = weights[9 * a + 3 * b + c, rows, :] * field_edge[c, rows, :]
+                    part = term if part is None else part + term
+                along_y.append(part)
+            along_z.append(
+                along_y[1] + (pltpu.roll(along_y[0], 2, 1) + pltpu.roll(along_y[2], LANES - 2, 1))
+            )
+        part = along_z[1] + (pltpu.roll(along_z[0], 12, 1) + pltpu.roll(along_z[2], LANES - 12, 1))
+        mixed_edge[rows, :] = part.astype(BF16)
+    first.middle()
+    make_mixed(-1)
+    make_mixed(2)
+    first.final()
+    wait_row(2)
+    wait_edges(1)
     edge_t[3] = placed(1, 1)
     edge_g[...] = dot_nt(eye, edge_t[3]).astype(BF16)
-    spread_edge = []
-    for a in range(3):
-        for b in range(3):
-            part = None
-            for c in range(3):
-                term = weights[9 * a + 3 * b + c] * field_edge[c]
-                part = term if part is None else part + term
-            step = 12 * (a - 1) + 2 * (b - 1)
-            spread_edge.append(pltpu.roll(part, (LANES - step) % LANES, 1))
-    mixed_edge[...] = sum(spread_edge[1:], spread_edge[0]).astype(BF16)
-    make_mixed(-1)
-    first.middle()
-    make_mixed(2)
-    wait_row(2)
-    first.final()
     first.finish()
 
     for i in range(n_bulk):
@@ -495,33 +578,30 @@
 
         conv(grads, y, weights, True, sink)
 
-    weight = jnp.zeros((C3, C), F32)
-    for y in range(2):
-        for z in range(4):
-            weight = weight + dot_nt(field_grad[y, z], x_ref[y, z])
-    pay2[:, 0:C] = weight
-
     def depth(j, carry):
-        rows = pl.ds(pl.multiple_of(j * DEPTH_CHUNK, DEPTH_CHUNK), DEPTH_CHUNK)
-        lane = iota((DEPTH_CHUNK, LANES), 1)
-        made = pay2[rows, :]
-        mine = [[grads[1, y + 1, z, rows, :] for z in range(4)] for y in range(2)]
+        rows = pl.ds(pl.multiple_of(j * CHUNK, CHUNK), CHUNK)
+        lane = iota((CHUNK, LANES), 1)
+        made = jnp.zeros((CHUNK, LANES), F32)
+        weight = jnp.zeros((CHUNK, C), F32)
+        for y in range(2):
+            for z in range(4):
+                weight = weight + dot_nt(field_grad[y, z, rows, :], x_ref[y, z])
         for b in range(3):
             for c in range(3):
-                cells = [[field[c, y + b + 1, z, rows, :] for z in range(4)] for y in range(2)]
                 for a in range(3):
                     total = None
                     for y in range(2):
                         for z in range(4):
                             if 0 <= z + a - 1 < 4:
-                                term = mine[y][z] * cells[y][z + a - 1]
+                                term = grads[1, y + 1, z, rows, :] * field[c, y + b + 1, z + a - 1, rows, :]
                                 total = term if total is None else total + term
                     tap = 9 * a + 3 * b + c
                     made = jnp.where(lane == C + tap, jnp.sum(total, axis=1, keepdims=True), made)
-        pay2[rows, :] = jnp.where(lane < C + 27, made, 0.0)
+        pay2[rows, :] = made
+        pay2[rows, 0:C] = weight
         return carry
 
-    lax.fori_loop(0, C3 // DEPTH_CHUNK, depth, 0)
+    lax.fori_loop(0, C3 // CHUNK, depth, 0)
     rows2 = C3 // n_bulk
     for i in range(n_bulk):
         pack2[i] = pay2[rows2 * i : rows2 * (i + 1), :]
@@ -533,9 +613,9 @@
     for k in range(3):
         pl.when(high)(lambda k=k: row_copy(k, True).wait_send())
         pl.when(low)(lambda k=k: row_copy(k, False).wait_send())
-    for (a, b) in NEIGHBOURS:
-        if (a, b) != (0, 0):
-            pl.when(inside(a, b))(lambda a=a, b=b: edge_copy(a, b).wait_send())
+    for kind in range(2):
+        for (a, b) in around:
+            pl.when(inside(a, b))(lambda a=a, b=b, kind=kind: edge_copy(kind, a, b).wait_send())
     first.drain()
     second.middle()
     second.final()
@@ -564,6 +644,7 @@
     place, flags = edge_tables()
     vmem = pl.BlockSpec(memory_space=pltpu.VMEM)
     smem = pl.BlockSpec(memory_space=pltpu.SMEM)
+    hbm = pl.BlockSpec(memory_space=pl.ANY)
     rows1, rows2 = C // n_bulk, C3 // n_bulk
 
     def reduction(rows):
@@ -586,15 +667,21 @@
             jax.ShapeDtypeStruct((27, C3), F32),
             jax.ShapeDtypeStruct((2,), F32),
         ),
-        in_specs=[vmem, vmem, vmem, vmem, smem, vmem, vmem],
+        in_specs=[hbm, hbm, hbm, hbm, smem, hbm, vmem],
         out_specs=(vmem, vmem, vmem, smem),
         scratch_shapes=[
+            pltpu.VMEM(x.shape, BF16),
+            pltpu.VMEM(g.shape, BF16),
+            pltpu.VMEM(w.shape, BF16),
+            pltpu.VMEM((27, C3), F32),
+            pltpu.VMEM(place.shape, BF16),
+            pltpu.SemaphoreType.DMA((5,)),
             pltpu.VMEM((2, 4, C, LANES), BF16),
             pltpu.VMEM((2, 4, C, LANES), BF16),
             pltpu.VMEM((4, 4, C, LANES), BF16),
             pltpu.VMEM((2, 4, C, LANES), BF16),
             pltpu.VMEM((2, 32, LANES), BF16),
-            pltpu.VMEM((9, 2, 32, LANES), BF16),
+            pltpu.VMEM((2, 9, 32, LANES), BF16),
             pltpu.VMEM((4, LANES, LANES), BF16),
             pltpu.VMEM((LANES, LANES), F32),
             pltpu.VMEM((LANES, LANES), BF16),
@@ -609,6 +696,7 @@
             pltpu.VMEM((C3, LANES), F32),
             pltpu.VMEM((2, 4, C3, LANES), BF16),
             pltpu.VMEM((LANES, LANES), F32),
+            pltpu.VMEM((2, 4, C3, LANES), F32),
             pltpu.VMEM((3, C, LANES), BF16),
             pltpu.VMEM((2, C, LANES), F32),
             pltpu.VMEM((C, LANES), F32),
@@ -616,7 +704,7 @@
         ]
         + reduction(rows1)
         + reduction(rows2)
-        + [dma(6), dma(6), dma(9), dma(9)]
+        + [dma(6), dma(6), dma(18), dma(18)]
         + reduction_sems
         + reduction_sems,
         compiler_params=pltpu.CompilerParams(

time: 58.8 us -> 56.8 us (0.966)
  Pallas kernels: 58 us -> 56 us
    pallas_call x1, Pallas kernels: 56.2 us -> 54.2 us  [local(): pl.pallas_call(functools.partial(kernel, (n_col, n_bulk), scale), out_sha...]
where the time goes in v4:
time: 56.8 us; the launch traced here: 56.6 us
  Pallas kernels  56 us (99%)
  between operations  0.64 us (1%)
    pallas_call x1, Pallas kernels, local(): pl.pallas_call(functools.partial(kernel, (n_col, n_bulk), scale), out_sha...  54.2 us
    pallas_call x1, Pallas kernels, local(): pl.pallas_call(hand_out, out_shape=tuple((jax.ShapeDtypeStruct(v.shape, v...  1.76 us

profile of v4, /device:TPU:1, one launch (start us, length us, event | category | flops | bytes accessed | tf_op | source)
XLA Modules:
  0.0 56.6 jit_solution(15378118441363911934)
XLA Ops:
  0.6 54.2 %shard_map.102 = (bf16[96,4,2,128]{3,2,1,0:T(2,128)(2,1)}, f32[288,96]{1,0:T(8,128)}, f32[27,288]{1,0:T(8,128)}, f32[2]{0:T(128)}) custom-call(bf16[96,4,2,128]{3,2,1,0:T(2,128)(2,1)} %x_hbm.1, bf16[96,4,2,128]{3,2,1,0:T(2,128)(2,1)} %g_hbm.1, bf16[288,96]{1,0:T(8,128)(2,1)} %w_hbm.1, f32[27,288]{1,0:T(8,128)} %bitcast.2, f32[2]{0:T(128)} %sharp_ref.1, ...), custom_call_target="tpu_custom_call" | custom-call | tf_op jit(solution)/shard_map/pallas_call | solution.py:662
  54.8 1.8 %shard_map.103 = (bf16[96,4,2,128]{3,2,1,0:T(2,128)(2,1)}, f32[288,96]{1,0:T(8,128)}, f32[27,288]{1,0:T(8,128)}, f32[2]{0:T(128)}) custom-call(bf16[96,4,2,128]{3,2,1,0:T(2,128)(2,1)} %get-tuple-element.12.dx_in, f32[288,96]{1,0:T(8,128)} %get-tuple-element.13.pd_in, f32[27,288]{1,0:T(8,128)} %get-tuple-element.14.kd_in, f32[2]{0:T(128)} %get-tuple-element.15.sd_in), custom_call_target="tpu_custom_call" | custom-call | tf_op jit(solution)/shard_map/pallas_call | solution.py:722

commit v5 on v4

--- a/solution.py
+++ b/solution.py
@@ -189,7 +189,6 @@
     dx_ref,
     pd_ref,
     kd_ref,
-    sd_ref,
     x_in,
     g_in,
     w_ref,
@@ -248,8 +247,8 @@
             ((x_hbm, x_in), (g_hbm, g_in), (w_hbm, w_ref), (k_hbm, k_ref), (place_hbm, place_ref))
         )
     ]
-    for load in loads:
-        load.start()
+    for i in (3, 0, 2, 1, 4):
+        loads[i].start()
 
     xh[...] = jnp.zeros_like(xh)
     gh[...] = jnp.zeros_like(gh)
@@ -259,14 +258,26 @@
     def greet(target):
         pl.semaphore_signal(barrier, inc=1, device_id=target, device_id_type=MESH)
 
+    for peer in peers[0][:10]:
+        greet((col, peer))
+    for peer in peers[1]:
+        greet((peer, bulk))
     for a in (1, n_col - 1):
         for b in (1, n_bulk - 1):
             greet((lax.rem(col + a, n_col), lax.rem(bulk + b, n_bulk)))
-    for peer in reversed(peers[1]):
-        greet((peer, bulk))
-    for peer in reversed(peers[0]):
+    for peer in peers[0][10:]:
         greet((col, peer))
-
+    loads[3].wait()
+    taps_t[...] = jnp.zeros_like(taps_t)
+    taps_t[0:27, 0:C3] = k_ref[...]
+    for j in range(3):
+        taps_c[LANES * j : LANES * (j + 1), :] = taps_t[:, LANES * j : LANES * (j + 1)].T
+
+    def spread_taps(which):
+        for t in which:
+            weights[t] = jnp.broadcast_to(taps_c[0:C3, t : t + 1], (C3, LANES))
+
+    spread_taps(range(EARLY_TAPS))
     row32, lane32 = iota((32, LANES), 0), iota((32, LANES), 1)
 
     def take_in(kind):
@@ -292,17 +303,6 @@
     take_in(0)
     make_messages(0)
 
-    loads[3].wait()
-    taps_t[...] = jnp.zeros_like(taps_t)
-    taps_t[0:27, 0:C3] = k_ref[...]
-    for j in range(3):
-        taps_c[LANES * j : LANES * (j + 1), :] = taps_t[:, LANES * j : LANES * (j + 1)].T
-
-    def spread_taps(which):
-        for t in which:
-            weights[t] = jnp.broadcast_to(taps_c[0:C3, t : t + 1], (C3, LANES))
-
-    spread_taps(range(EARLY_TAPS))
     pl.semaphore_wait(barrier, n_bulk + n_col - 2 + 4)
 
     def row_copy(k, down):
@@ -508,8 +508,9 @@
     attention = numerators / jnp.sum(numerators, axis=1, keepdims=True)
     score = attention * (value - jnp.sum(attention * value, axis=1, keepdims=True))
     by_cosine = score * cosine
-    sd_ref[0] = jnp.sum(jnp.where(upper, by_cosine, 0.0)) * scale
-    sd_ref[1] = jnp.sum(jnp.where(upper, 0.0, by_cosine)) * scale
+    for e in range(2):
+        total = jnp.sum(jnp.where(upper if e == 0 else ~upper, by_cosine, 0.0), axis=1, keepdims=True)
+        kd_ref[27 + e : 28 + e, :] = jnp.broadcast_to(jnp.sum(total, axis=0, keepdims=True) * scale, (1, C3))
     cosine_grad = sharp * score
     diagonal = cosine_grad * cosine
     diag_q = jnp.sum(diagonal, axis=1, keepdims=True)
@@ -626,16 +627,16 @@
     taps_c[0:C3, :] = pay2[...] * scale
     for j in range(3):
         taps_t[:, LANES * j : LANES * (j + 1)] = taps_c[LANES * j : LANES * (j + 1), :].T
-    kd_ref[...] = taps_t[C : C + 27, 0:C3]
+    kd_ref[0:27, :] = taps_t[C : C + 27, 0:C3]
     second.drain()
 
 
-def hand_out(dx_in, pd_in, kd_in, sd_in, dx_ref, pd_ref, kd_ref, sd_ref):
+def hand_out(dx_in, pd_in, kd_in, dx_ref, pd_ref, kd_ref, sd_ref):
     dx_ref[...] = dx_in[...]
     pd_ref[...] = pd_in[...]
-    kd_ref[...] = kd_in[...]
+    kd_ref[...] = kd_in[0:27, :]
     for e in range(2):
-        sd_ref[e] = sd_in[e]
+        sd_ref[e] = kd_in[27 + e, 0]
 
 
 def local(x, g, w, k, sharp):
@@ -659,16 +660,15 @@
         return pltpu.SemaphoreType.DMA((count,))
 
     reduction_sems = [pltpu.SemaphoreType.DMA] * 6
-    dx, pd, kd, sd = pl.pallas_call(
+    dx, pd, kd = pl.pallas_call(
         functools.partial(kernel, (n_col, n_bulk), scale),
         out_shape=(
-            jax.ShapeDtypeStruct((C, 4, 2, LANES), BF16),
-            jax.ShapeDtypeStruct((C3, C), F32),
-            jax.ShapeDtypeStruct((27, C3), F32),
-            jax.ShapeDtypeStruct((2,), F32),
+            pltpu.VMEM((C, 4, 2, LANES), BF16),
+            pltpu.VMEM((C3, C), F32),
+            pltpu.VMEM((32, C3), F32),
         ),
         in_specs=[hbm, hbm, hbm, hbm, smem, hbm, vmem],
-        out_specs=(vmem, vmem, vmem, smem),
+        out_specs=(vmem, vmem, vmem),
         scratch_shapes=[
             pltpu.VMEM(x.shape, BF16),
             pltpu.VMEM(g.shape, BF16),
@@ -721,10 +721,16 @@
     )
     dx, pd, kd, sd = pl.pallas_call(
         hand_out,
-        out_shape=tuple(jax.ShapeDtypeStruct(v.shape, v.dtype) for v in (dx, pd, kd, sd)),
-        in_specs=[vmem, vmem, vmem, smem],
+        out_shape=(
+            jax.ShapeDtypeStruct((C, 4, 2, LANES), BF16),
+            jax.ShapeDtypeStruct((C3, C), F32),
+            jax.ShapeDtypeStruct((27, C3), F32),
+            jax.ShapeDtypeStruct((2,), F32),
+        ),
+        in_specs=[vmem, vmem, vmem],
         out_specs=(vmem, vmem, vmem, smem),
-    )(dx, pd, kd, sd)
+        compiler_params=pltpu.CompilerParams(vmem_limit_bytes=4 * 2**20),
+    )(dx, pd, kd)
     return dx, pd, kd.T, sd
 
 

time: 56.8 us -> 54.9 us (0.967)
  Pallas kernels: 56 us -> 54.2 us
    pallas_call x1, Pallas kernels: 1.76 us -> 0.77 us  [local(): pl.pallas_call(hand_out, out_shape=(jax.ShapeDtypeStruct((C, 4, 2, LANES)...]
    pallas_call x1, Pallas kernels: 54.2 us -> 53.4 us  [local(): pl.pallas_call(functools.partial(kernel, (n_col, n_bulk), scale), out_sha...]
where the time goes in v5:
time: 54.9 us; the launch traced here: 54.8 us
  Pallas kernels  54.2 us (99%)
  between operations  0.64 us (1%)
    pallas_call x1, Pallas kernels, local(): pl.pallas_call(functools.partial(kernel, (n_col, n_bulk), scale), out_sha...  53.4 us

profile of v5, /device:TPU:1, one launch (start us, length us, event | category | flops | bytes accessed | tf_op | source)
XLA Modules:
  0.0 54.8 jit_solution(10734687209778915728)
XLA Ops:
  0.6 53.4 %shard_map.102 = (bf16[96,4,2,128]{3,2,1,0:T(2,128)(2,1)S(1)}, f32[288,96]{1,0:T(8,128)S(1)}, f32[32,288]{1,0:T(8,128)S(1)}) custom-call(bf16[96,4,2,128]{3,2,1,0:T(2,128)(2,1)} %x_hbm.1, bf16[96,4,2,128]{3,2,1,0:T(2,128)(2,1)} %g_hbm.1, bf16[288,96]{1,0:T(8,128)(2,1)} %w_hbm.1, f32[27,288]{1,0:T(8,128)} %bitcast.2, f32[2]{0:T(128)} %sharp_ref.1, ...), custom_call_target="tpu_custom_call" | custom-call | tf_op jit(solution)/shard_map/pallas_call | solution.py:663
  54.0 0.8 %shard_map.103 = (bf16[96,4,2,128]{3,2,1,0:T(2,128)(2,1)}, f32[288,96]{1,0:T(8,128)}, f32[27,288]{1,0:T(8,128)}, f32[2]{0:T(128)}) custom-call(bf16[96,4,2,128]{3,2,1,0:T(2,128)(2,1)S(1)} %get-tuple-element.11.dx_in, f32[288,96]{1,0:T(8,128)S(1)} %get-tuple-element.12.pd_in, f32[32,288]{1,0:T(8,128)S(1)} %get-tuple-element.13.kd_in), custom_call_target="tpu_custom_call" | custom-call | tf_op jit(solution)/shard_map/pallas_call | solution.py:722

commit v6 on v5

--- a/solution.py
+++ b/solution.py
@@ -17,6 +17,7 @@
 C3 = 3 * C
 LANES = 128
 CHUNK = 32
+DEPTH_CHUNK = 96
 EARLY_TAPS = 10
 EDGE_COLUMNS = (0, 1, LANES - 2, LANES - 1)
 NEIGHBOURS = [(a, b) for a in (-1, 0, 1) for b in (-1, 0, 1)]
@@ -156,8 +157,7 @@
 
 
 def conv(source, y0, weights, flip, sink, bs=(0, 1, 2), start=None):
-    def body(j, carry):
-        rows = pl.ds(pl.multiple_of(j * CHUNK, CHUNK), CHUNK)
+    def chunk(rows):
         total = [None if start is None else start(z, rows) for z in range(4)]
         for b in bs:
             for c in range(3):
@@ -171,9 +171,13 @@
                             total[z] = term if total[z] is None else total[z] + term
         for z in range(4):
             sink(z, rows, total[z])
+
+    def body(j, carry):
+        for h in range(3):
+            chunk(pl.ds(pl.multiple_of(j * 3 * CHUNK + h * CHUNK, CHUNK), CHUNK))
         return carry
 
-    lax.fori_loop(0, C3 // CHUNK, body, 0)
+    lax.fori_loop(0, C3 // (3 * CHUNK), body, 0)
 
 
 def kernel(
@@ -351,8 +355,8 @@
 
     def shifted(values, edge):
         lane = iota(values.shape, 1)
-        before = jnp.where(lane == 0, edge, pltpu.roll(values, 1, 1))
-        after = jnp.where(lane == LANES - 1, edge, pltpu.roll(values, LANES - 1, 1))
+        before = jnp.where(lane == 0, edge, pltpu.roll(values, 1, 1).astype(F32))
+        after = jnp.where(lane == LANES - 1, edge, pltpu.roll(values, LANES - 1, 1).astype(F32))
         return before, after
 
     def input_row(y):
@@ -362,9 +366,8 @@
         for y in ys:
             for z in range(4):
                 plane = input_row(y)[z]
-                wide = plane.astype(F32)
-                edge = turned(edge_x[0:C, :], z, y) if edged else 0.0
-                before, after = shifted(wide, edge)
+                edge = turned(edge_x[0:C, :], z, y).astype(F32) if edged else 0.0
+                before, after = shifted(plane, edge)
                 cells = jnp.concatenate([before.astype(BF16), plane, after.astype(BF16)], axis=1)
                 made = rounded(dot(w_ref[...], cells))
                 for c in range(3):
@@ -456,11 +459,11 @@
     make_messages(1)
     send_edges(1)
     wait_row(1)
-    edge_x[...] = dot_nt(eye, edge_t[1])
+    edge_x[...] = dot_nt(eye, edge_t[1]).astype(BF16)
     make_field((-2, 3), True)
     for y in range(-1, 3):
         for z in range(4):
-            edge = turned(field_edge[1], z, y)
+            edge = turned(field_edge[1].astype(BF16), z, y).astype(F32)
             field[0, y + 2, z, :, 0:1] = edge[:, 0:1]
             field[2, y + 2, z, :, LANES - 1 : LANES] = edge[:, LANES - 1 : LANES]
     for c in (0, 2):
@@ -508,9 +511,7 @@
     attention = numerators / jnp.sum(numerators, axis=1, keepdims=True)
     score = attention * (value - jnp.sum(attention * value, axis=1, keepdims=True))
     by_cosine = score * cosine
-    for e in range(2):
-        total = jnp.sum(jnp.where(upper if e == 0 else ~upper, by_cosine, 0.0), axis=1, keepdims=True)
-        kd_ref[27 + e : 28 + e, :] = jnp.broadcast_to(jnp.sum(total, axis=0, keepdims=True) * scale, (1, C3))
+    pay1[...] = by_cosine
     cosine_grad = sharp * score
     diagonal = cosine_grad * cosine
     diag_q = jnp.sum(diagonal, axis=1, keepdims=True)
@@ -521,16 +522,16 @@
             upper, jnp.where(inner, v, 0.0), jnp.where((lane >= HEAD) & (lane < C), pltpu.roll(v, HEAD, 1), 0.0)
         )
 
-    def transposed(v):
-        turn[0:C, :] = v
-        turn[C:LANES, :] = jnp.zeros((LANES - C, LANES), F32)
-        return turn[...].T
+    def transposed(k, v):
+        turn[k, 0:C, :] = v
+        turn[k, C:LANES, :] = jnp.zeros((LANES - C, LANES), F32)
+        return turn[k].T
 
     coupled = blocks(coupling)
     couple[0] = coupled.astype(BF16)
-    couple[1] = transposed(coupled)[0:C, :].astype(BF16)
-    couple[2] = transposed(blocks(attention))[0:C, :].astype(BF16)
-    diag_k = jnp.sum(transposed(blocks(diagonal)), axis=1, keepdims=True)[0:C, :]
+    couple[1] = transposed(0, coupled)[0:C, :].astype(BF16)
+    couple[2] = transposed(1, blocks(attention))[0:C, :].astype(BF16)
+    diag_k = jnp.sum(transposed(2, blocks(diagonal)), axis=1, keepdims=True)[0:C, :]
     coef[0] = jnp.broadcast_to(inv_q * inv_q * diag_q, (C, LANES))
     coef[1] = jnp.broadcast_to(inv_k * inv_k * diag_k, (C, LANES))
 
@@ -551,7 +552,7 @@
     )
     edges = gradients(mixed_edge[0:C, :], mixed_edge[C : 2 * C, :], edge_g[0:C, :])
     for part in range(3):
-        grads_edge[C * part : C * (part + 1), :] = jnp.where(mask > 0.5, rounded(edges[part]), 0.0)
+        grads_edge[C * part : C * (part + 1), :] = jnp.where(mask > 0.5, edges[part], 0.0).astype(BF16)
 
     def grad_planes(z):
         for y in range(-1, 3):
@@ -564,7 +565,10 @@
                     plane = plane * flag(low)
                 if y == 2:
                     plane = plane * flag(high)
-                before, after = shifted(plane, turned(grads_edge[rows, :], z, y))
+                edge = turned(grads_edge[rows, :], z, y).astype(F32)
+                narrow = plane.astype(BF16)
+                before = jnp.where(lane == 0, edge, pltpu.roll(narrow, 1, 1).astype(F32))
+                after = jnp.where(lane == LANES - 1, edge, pltpu.roll(narrow, LANES - 1, 1).astype(F32))
                 grads[0, y + 1, z, rows, :] = before
                 grads[1, y + 1, z, rows, :] = plane
                 grads[2, y + 1, z, rows, :] = after
@@ -580,34 +584,42 @@
         conv(grads, y, weights, True, sink)
 
     def depth(j, carry):
-        rows = pl.ds(pl.multiple_of(j * CHUNK, CHUNK), CHUNK)
-        lane = iota((CHUNK, LANES), 1)
-        made = jnp.zeros((CHUNK, LANES), F32)
-        weight = jnp.zeros((CHUNK, C), F32)
+        group = pl.ds(pl.multiple_of(j * DEPTH_CHUNK, DEPTH_CHUNK), DEPTH_CHUNK)
+        weight = jnp.zeros((DEPTH_CHUNK, C), F32)
         for y in range(2):
             for z in range(4):
-                weight = weight + dot_nt(field_grad[y, z, rows, :], x_ref[y, z])
-        for b in range(3):
-            for c in range(3):
-                for a in range(3):
-                    total = None
-                    for y in range(2):
-                        for z in range(4):
-                            if 0 <= z + a - 1 < 4:
-                                term = grads[1, y + 1, z, rows, :] * field[c, y + b + 1, z + a - 1, rows, :]
-                                total = term if total is None else total + term
-                    tap = 9 * a + 3 * b + c
-                    made = jnp.where(lane == C + tap, jnp.sum(total, axis=1, keepdims=True), made)
-        pay2[rows, :] = made
-        pay2[rows, 0:C] = weight
+                weight = weight + dot_nt(field_grad[y, z, group, :], x_ref[y, z])
+        lane = iota((16, LANES), 1)
+        for h in range(DEPTH_CHUNK // 16):
+            rows = pl.ds(pl.multiple_of(j * DEPTH_CHUNK + 16 * h, 16), 16)
+            made = jnp.zeros((16, LANES), F32)
+            mine = [[grads[1, y + 1, z, rows, :] for z in range(4)] for y in range(2)]
+            for b in range(3):
+                for c in range(3):
+                    cells = [[field[c, y + b + 1, z, rows, :] for z in range(4)] for y in range(2)]
+                    for a in range(3):
+                        total = None
+                        for y in range(2):
+                            for z in range(4):
+                                if 0 <= z + a - 1 < 4:
+                                    term = mine[y][z] * cells[y][z + a - 1]
+                                    total = term if total is None else total + term
+                        tap = 9 * a + 3 * b + c
+                        made = jnp.where(lane == C + tap, jnp.sum(total, axis=1, keepdims=True), made)
+            pay2[rows, :] = made
+        pay2[group, 0:C] = weight
         return carry
 
-    lax.fori_loop(0, C3 // CHUNK, depth, 0)
+    lax.fori_loop(0, C3 // DEPTH_CHUNK, depth, 0)
     rows2 = C3 // n_bulk
     for i in range(n_bulk):
         pack2[i] = pay2[rows2 * i : rows2 * (i + 1), :]
     second.start()
 
+    by_cosine = pay1[...]
+    for e in range(2):
+        total = jnp.sum(jnp.where(upper if e == 0 else ~upper, by_cosine, 0.0), axis=1, keepdims=True)
+        kd_ref[27 + e : 28 + e, :] = jnp.broadcast_to(jnp.sum(total, axis=0, keepdims=True) * scale, (1, C3))
     for z in range(4):
         rows_y = [dot_tn(w_ref[...], field_grad[y, z]) for y in range(2)]
         dx_ref[:, z] = jnp.stack(rows_y, axis=1).astype(BF16)
@@ -683,7 +695,7 @@
             pltpu.VMEM((2, 32, LANES), BF16),
             pltpu.VMEM((2, 9, 32, LANES), BF16),
             pltpu.VMEM((4, LANES, LANES), BF16),
-            pltpu.VMEM((LANES, LANES), F32),
+            pltpu.VMEM((LANES, LANES), BF16),
             pltpu.VMEM((LANES, LANES), BF16),
             pltpu.VMEM((LANES, 3 * LANES), F32),
             pltpu.VMEM((3 * LANES, LANES), F32),
@@ -693,9 +705,9 @@
             pltpu.VMEM((4, 4, C3, LANES), BF16),
             pltpu.VMEM((C3, LANES), BF16),
             pltpu.VMEM((3, 4, 4, C3, LANES), F32),
-            pltpu.VMEM((C3, LANES), F32),
+            pltpu.VMEM((C3, LANES), BF16),
             pltpu.VMEM((2, 4, C3, LANES), BF16),
-            pltpu.VMEM((LANES, LANES), F32),
+            pltpu.VMEM((3, LANES, LANES), F32),
             pltpu.VMEM((2, 4, C3, LANES), F32),
             pltpu.VMEM((3, C, LANES), BF16),
             pltpu.VMEM((2, C, LANES), F32),

time: 54.9 us -> 53.6 us (0.976)
  Pallas kernels: 54.2 us -> 52.9 us
    pallas_call x1, Pallas kernels: 53.4 us -> 52.1 us  [local(): pl.pallas_call(functools.partial(kernel, (n_col, n_bulk), scale), out_sha...]
where the time goes in v6:
time: 53.6 us; the launch traced here: 53.5 us
  Pallas kernels  52.9 us (99%)
  between operations  0.64 us (1%)
    pallas_call x1, Pallas kernels, local(): pl.pallas_call(functools.partial(kernel, (n_col, n_bulk), scale), out_sha...  52.1 us

profile of v6, /device:TPU:1, one launch (start us, length us, event | category | flops | bytes accessed | tf_op | source)
XLA Modules:
  0.0 53.5 jit_solution(5674234480430121824)
XLA Ops:
  0.6 52.1 %shard_map.102 = (bf16[96,4,2,128]{3,2,1,0:T(2,128)(2,1)S(1)}, f32[288,96]{1,0:T(8,128)S(1)}, f32[32,288]{1,0:T(8,128)S(1)}) custom-call(bf16[96,4,2,128]{3,2,1,0:T(2,128)(2,1)} %x_hbm.1, bf16[96,4,2,128]{3,2,1,0:T(2,128)(2,1)} %g_hbm.1, bf16[288,96]{1,0:T(8,128)(2,1)} %w_hbm.1, f32[27,288]{1,0:T(8,128)} %bitcast.2, f32[2]{0:T(128)} %sharp_ref.1, ...), custom_call_target="tpu_custom_call" | custom-call | tf_op jit(solution)/shard_map/pallas_call | solution.py:675
  52.7 0.8 %shard_map.103 = (bf16[96,4,2,128]{3,2,1,0:T(2,128)(2,1)}, f32[288,96]{1,0:T(8,128)}, f32[27,288]{1,0:T(8,128)}, f32[2]{0:T(128)}) custom-call(bf16[96,4,2,128]{3,2,1,0:T(2,128)(2,1)S(1)} %get-tuple-element.11.dx_in, f32[288,96]{1,0:T(8,128)S(1)} %get-tuple-element.12.pd_in, f32[32,288]{1,0:T(8,128)S(1)} %get-tuple-element.13.kd_in), custom_call_target="tpu_custom_call" | custom-call | tf_op jit(solution)/shard_map/pallas_call | solution.py:734

commit v7 on v6

--- a/solution.py
+++ b/solution.py
@@ -156,8 +156,8 @@
         self.gathered().wait_send()
 
 
-def conv(source, y0, weights, flip, sink, bs=(0, 1, 2), start=None):
-    def chunk(rows):
+def conv(source, weights, flip, jobs):
+    def chunk(rows, y0, sink, bs=(0, 1, 2), start=None):
         total = [None if start is None else start(z, rows) for z in range(4)]
         for b in bs:
             for c in range(3):
@@ -174,7 +174,8 @@
 
     def body(j, carry):
         for h in range(3):
-            chunk(pl.ds(pl.multiple_of(j * 3 * CHUNK + h * CHUNK, CHUNK), CHUNK))
+            for job in jobs:
+                chunk(pl.ds(pl.multiple_of(j * 3 * CHUNK + h * CHUNK, CHUNK), CHUNK), *job)
         return carry
 
     lax.fori_loop(0, C3 // (3 * CHUNK), body, 0)
@@ -373,32 +374,41 @@
                 for c in range(3):
                     field[c, y + 2, z] = made[:, LANES * c : LANES * (c + 1)]
 
-    def gather(y, bs, start):
-        def sink(z, rows, value):
-            partial[y, z, rows, :] = value
-
-        conv(field, y + 1, weights, False, sink, bs, start)
-
-    def make_mixed(y):
-        def sink(z, rows, value):
-            mixed[y + 1, z, rows, :] = value.astype(BF16)
-
-        conv(field, y + 1, weights, False, sink)
+    def gather(parts):
+        def job(y, bs, start):
+            def sink(z, rows, value):
+                partial[y, z, rows, :] = value
+
+            return y + 1, sink, bs, start
+
+        conv(field, weights, False, [job(*part) for part in parts])
+
+    def make_mixed(ys):
+        def job(y):
+            def sink(z, rows, value):
+                mixed[y + 1, z, rows, :] = value.astype(BF16)
+
+            return y + 1, sink
+
+        conv(field, weights, False, [job(y) for y in ys])
 
     for load in (loads[2], loads[4]):
         load.wait()
     spread_taps(range(EARLY_TAPS, 27))
 
     make_field((0, 1), False)
-    gather(0, (1, 2), None)
-    gather(1, (0, 1), None)
+    gather([(0, (1, 2), None), (1, (0, 1), None)])
     take_in(1)
     wait_row(0)
     for k in (1, 2):
         send_row(k)
     make_field((-1, 2), False)
-    gather(0, (0,), lambda z, rows: partial[0, z, rows, :])
-    gather(1, (2,), lambda z, rows: partial[1, z, rows, :])
+    gather(
+        [
+            (0, (0,), lambda z, rows: partial[0, z, rows, :]),
+            (1, (2,), lambda z, rows: partial[1, z, rows, :]),
+        ]
+    )
     wait_edges(0)
 
     def placed(c, kind):
@@ -414,7 +424,8 @@
     for j in range(3):
         rows = slice(C * j, C * (j + 1))
         beside = field_edge[1, rows, :]
-        along_y = [pltpu.roll(beside, 2, 1), beside, pltpu.roll(beside, LANES - 2, 1)]
+        narrow = beside.astype(BF16)
+        along_y = [pltpu.roll(narrow, 2, 1).astype(F32), beside, pltpu.roll(narrow, LANES - 2, 1).astype(F32)]
         along_z = []
         for a in range(3):
             part = None
@@ -486,8 +497,7 @@
         part = along_z[1] + (pltpu.roll(along_z[0], 12, 1) + pltpu.roll(along_z[2], LANES - 12, 1))
         mixed_edge[rows, :] = part.astype(BF16)
     first.middle()
-    make_mixed(-1)
-    make_mixed(2)
+    make_mixed((-1, 2))
     first.final()
     wait_row(2)
     wait_edges(1)
@@ -576,12 +586,13 @@
     for z in range(4):
         grad_planes(z)
 
-    for y in range(2):
-
-        def sink(z, rows, value, y=y):
+    def spread(y):
+        def sink(z, rows, value):
             field_grad[y, z, rows, :] = value.astype(BF16)
 
-        conv(grads, y, weights, True, sink)
+        return y, sink
+
+    conv(grads, weights, True, [spread(y) for y in range(2)])
 
     def depth(j, carry):
         group = pl.ds(pl.multiple_of(j * DEPTH_CHUNK, DEPTH_CHUNK), DEPTH_CHUNK)

time: 53.6 us -> 53.6 us (level)
  no operation moved by 1% of the time
where the time goes in v7:
time: 53.6 us; the launch traced here: 53.5 us
  Pallas kernels  52.8 us (99%)
  between operations  0.64 us (1%)
    pallas_call x1, Pallas kernels, local(): pl.pallas_call(functools.partial(kernel, (n_col, n_bulk), scale), out_sha...  52 us

profile of v7, /device:TPU:1, one launch (start us, length us, event | category | flops | bytes accessed | tf_op | source)
XLA Modules:
  0.0 53.5 jit_solution(8561002639707829742)
XLA Ops:
  0.6 52.0 %shard_map.102 = (bf16[96,4,2,128]{3,2,1,0:T(2,128)(2,1)S(1)}, f32[288,96]{1,0:T(8,128)S(1)}, f32[32,288]{1,0:T(8,128)S(1)}) custom-call(bf16[96,4,2,128]{3,2,1,0:T(2,128)(2,1)} %x_hbm.1, bf16[96,4,2,128]{3,2,1,0:T(2,128)(2,1)} %g_hbm.1, bf16[288,96]{1,0:T(8,128)(2,1)} %w_hbm.1, f32[27,288]{1,0:T(8,128)} %bitcast.2, f32[2]{0:T(128)} %sharp_ref.1, ...), custom_call_target="tpu_custom_call" | custom-call | tf_op jit(solution)/shard_map/pallas_call | solution.py:686
  52.7 0.8 %shard_map.103 = (bf16[96,4,2,128]{3,2,1,0:T(2,128)(2,1)}, f32[288,96]{1,0:T(8,128)}, f32[27,288]{1,0:T(8,128)}, f32[2]{0:T(128)}) custom-call(bf16[96,4,2,128]{3,2,1,0:T(2,128)(2,1)S(1)} %get-tuple-element.11.dx_in, f32[288,96]{1,0:T(8,128)S(1)} %get-tuple-element.12.pd_in, f32[32,288]{1,0:T(8,128)S(1)} %get-tuple-element.13.kd_in), custom_call_target="tpu_custom_call" | custom-call | tf_op jit(solution)/shard_map/pallas_call | solution.py:745
